TPU v7x, 32 devices: a whole 2x2x4 slice. The times are simulated.
32 devices in a mesh: clips: 2 (over y), tiles: 4 (over z), frames: 2 (over x), chan: 2 (over core).
Axes of the slice: x: 2, y: 2, z: 4, core: 2. Of those that a mesh axis runs over, the one named last changes fastest.
Arguments:
- lr_feats: bfloat16 [8, 2, 64, 32, 128], P('clips', 'frames', 'chan', 'tiles'), parts along dimension 0, may hold values from -6 to 6
- flow_prev: int32 [8, 2, 4, 2], P('clips', None, 'tiles'), parts along dimension 0, may hold values from -8 to 8, as said below
- flow_second: int32 [8, 2, 4, 2], P('clips', None, 'tiles'), parts along dimension 0, may hold values from -8 to 8, as said below
- w_join: bfloat16 [9, 64, 192], P(None, 'chan'), may hold values from -0.15625 to 0.15625
- b_join: float32 [64], P('chan'), may hold values from -3 to 3
- w_first: bfloat16 [1, 9, 64, 64], P(None, None, 'chan'), may hold values from -0.25 to 0.25
- b_first: float32 [1, 64], P(None, 'chan'), may hold values from -3 to 3
- w_second: bfloat16 [1, 9, 64, 64], P(None, None, 'chan'), may hold values from -0.25 to 0.25
- b_second: float32 [1, 64], P(None, 'chan'), may hold values from -3 to 3
Outputs:
- hidden: bfloat16 [8, 2, 64, 32, 128], P('clips', 'frames', 'chan', 'tiles'), parts along dimension 0
There are 2 independent parts, one for each index of `clips`. A program takes and returns all parts, laid end to end along the dimension named above; an argument that names none is the same for every part. Nothing has to cross between parts.
Inputs may be any that keep to these rules, and one draw needn't show every extreme that they name: `flow_prev`: both entries (dy, dx) of every block lie in the range; +8 and -8 each occur in every draw. `flow_second`: both entries (dy, dx) of every block lie in the range; +8 and -8 each occur in every draw.
All inputs are finite; a program needn't handle non-finite values.
Results may differ from a plain program's by a relative error of at most 0.012.
Values may be sent and summed in bfloat16 or wider, within the bound.
No kernel may reach another device: no remote copies, remote signals or barrier semaphores. Data moves between devices by JAX's collectives and lax.ppermute only.
A program may use at most 64 MiB of HBM per device.

v0:
```python
import functools
import math

import jax
import jax.numpy as jnp
from jax import lax
from jax.experimental import pallas as pl
from jax.experimental.pallas import tpu as pltpu
from jax.sharding import PartitionSpec as P


TAPS = 3
LANES = 128
TAIL = 8
PIECES = 3
UNROLL = 4
SPARE = 4 * 2**20
VMEM = pl.BlockSpec(memory_space=pltpu.VMEM)
HBM = pl.BlockSpec(memory_space=pltpu.HBM)


def partner(index, shift, count):
    return (index + shift) % count if isinstance(index, int) else lax.rem(index + shift, count)


def origin(index, shift, count):
    return lax.rem(index + count - shift, count)


def hop(array, axis, shift, stride=1):
    count = lax.axis_size(axis) // stride
    if shift == 0:
        return array
    pairs = [
        (i * stride + j, partner(i, shift, count) * stride + j)
        for i in range(count)
        for j in range(stride)
    ]
    return lax.ppermute(array, axis, pairs)


def ranked(count):
    return list(range(1, count))


def in_hbm(*arrays):
    return tuple(pltpu.with_memory_space_constraint(array, pltpu.HBM) for array in arrays)


def call(kernel, operands, out_shape, scratch, in_specs, out_specs):
    shapes = jax.tree.leaves((operands, out_shape))
    held = sum(
        shape.size * shape.dtype.itemsize
        for shape in shapes
    ) + sum(
        math.prod(item.shape) * jnp.dtype(item.dtype).itemsize
        for item in scratch
        if item.memory_space == pltpu.VMEM
    )
    return pl.pallas_call(
        kernel,
        out_shape=out_shape,
        in_specs=in_specs,
        out_specs=out_specs,
        scratch_shapes=scratch,
        compiler_params=pltpu.CompilerParams(vmem_limit_bytes=held + SPARE),
    )(*operands)


def split_of(segments, tiles):
    span = max(1, tiles // segments)
    groups = tiles // span
    return span, groups, segments // groups


def starts_of(widths):
    starts, at = [], 0
    for width in widths:
        starts.append(at)
        at += -(-TAPS * width // LANES) * LANES
    return starts + [at]


def pack(lr_feats, *rest):
    flows, rest = rest[:2], rest[2:]
    outs, rest = rest[:-5], rest[-5:]
    held, table_prev, table_second, stage, came = rest
    segments, _, part, depth, cols = lr_feats.shape
    frames = flows[0].shape[0]
    tiles = len(outs)
    span, _, count = split_of(segments, tiles)
    tile = lax.axis_index("tiles")
    tables = (table_prev, table_second)
    fetches = [
        pltpu.make_async_copy(flow, table, came.at[len(outs) * count + index])
        for index, (flow, table) in enumerate(zip(flows, tables))
    ]
    order = ranked(tiles) + [0]

    def first_of(shift):
        return partner(tile, shift, tiles) // span * count

    loads = {}
    for shift in order:
        for index in range(count):
            slot = shift * count + index
            loads[slot] = pltpu.make_async_copy(
                lr_feats.at[first_of(shift) + index, 0], held.at[slot], came.at[slot]
            )
            loads[slot].start()
    for fetch in fetches:
        fetch.start()
    lane = lax.broadcasted_iota(jnp.int32, (TAIL, cols), 1)
    for shift in order:
        for index in range(count):
            slot = shift * count + index
            loads[slot].wait()
            stage[slot] = held[slot].astype(jnp.float32).reshape(part * depth, cols)
            for row in range(depth):
                value = stage[slot, pl.ds(row, part, stride=depth), :]
                outs[shift][index, row * part : (row + 1) * part] = value.astype(jnp.bfloat16)
    for fetch in fetches:
        fetch.wait()
    for shift in order:
        for index in range(count):
            tail = jnp.zeros((TAIL, cols), jnp.int32)
            for which, table in enumerate(tables):
                for frame in range(frames):
                    for entry in range(2):
                        at = (which * frames + frame) * 2 + entry
                        number = table[frame, 0, entry, first_of(shift) + index]
                        tail = jnp.where(lane == at, number, tail)
            outs[shift][index, part * depth :] = tail.astype(jnp.float32).astype(jnp.bfloat16)


def unpack(*refs):
    blocks, out, left = refs[:-2], refs[-2], refs[-1]
    groups = len(blocks)
    count = out.shape[0] // groups
    span = lax.axis_size("tiles") // groups
    tile = lax.axis_index("tiles")
    copies = []
    for turn, block in enumerate(blocks):
        first = origin(tile // span, turn, groups) * count
        for index in range(count):
            copies.append(
                pltpu.make_async_copy(
                    block.at[index], out.at[first + index, 0], left.at[turn * count + index]
                )
            )
    for copy in copies:
        copy.start()
    for copy in copies:
        copy.wait()


def arrange(widths, *refs):
    count = len(widths)
    sources, out, rest = refs[: 2 * count], refs[2 * count], refs[2 * count + 1 :]
    copies = [
        pltpu.make_async_copy(source, held, rest[-1].at[index])
        for index, (source, held) in enumerate(zip(sources, rest))
    ]
    for copy in copies:
        copy.start()
    for copy in copies:
        copy.wait()
    weights, biases = rest[:count], rest[count : 2 * count]
    part = out.shape[0] // TAPS
    *starts, end = starts_of(widths)
    channels = min(widths)
    for weight, width, start in zip(weights, widths, starts):
        for row in range(TAPS):
            pieces = [
                weight[TAPS * row + col, :, source : source + channels]
                for source in range(0, width, channels)
                for col in range(TAPS)
            ]
            out[row * part : (row + 1) * part, start : start + TAPS * width] = jnp.concatenate(
                pieces, axis=1
            )
    square = (part, part)
    diagonal = lax.broadcasted_iota(jnp.int32, square, 0) == lax.broadcasted_iota(jnp.int32, square, 1)
    lane = lax.broadcasted_iota(jnp.int32, (part, LANES), 1)
    block = jnp.zeros((part, LANES), jnp.float32)
    for index, bias in enumerate(biases):
        rest = bias[...]
        for piece in range(PIECES):
            rounded = rest.astype(jnp.bfloat16).astype(jnp.float32)
            rest = rest - rounded
            spread = jnp.broadcast_to(rounded, square)
            column = jnp.sum(jnp.where(diagonal, spread, 0.0), axis=1, keepdims=True)
            block = jnp.where(lane == PIECES * index + piece, column, block)
    out[:part, end:] = block.astype(jnp.bfloat16)
    out[part:, end:] = jnp.zeros(((TAPS - 1) * part, LANES), jnp.bfloat16)


def moved(value, step):
    cols = value.shape[1]
    lane = lax.broadcasted_iota(jnp.int32, value.shape, 1)
    rolled = pltpu.roll(value, lax.rem(cols - step, cols), 1)
    return jnp.where((lane + step >= 0) & (lane + step < cols), rolled, jnp.zeros_like(rolled))


def taps(value):
    return jnp.concatenate([moved(value, -1), value, moved(value, 1)], axis=0)


def recurrence(sizes, widths, *refs):
    frames, tiles, chans, segments, part, depth, cols = sizes
    span, groups, count = split_of(segments, tiles)
    n_blocks = frames * tiles * chans
    sides, refs = refs[:chans], refs[chans:]
    blocks, refs = refs[:n_blocks], refs[n_blocks:]
    outs, refs = refs[:groups], refs[groups:]
    weights, numbers, table, features, joined, inner, history, stage = refs[:8]
    fetched, arrived, counted = refs[8:]
    channels = part * chans
    rows = tiles * depth
    tile, frame_here, chan = (lax.axis_index(name) for name in ("tiles", "frames", "chan"))
    kept = history.shape[0]
    top = depth + 1
    starts = starts_of(widths)

    def copy_in(segment, shift, index):
        frame = origin(frame_here, shift, frames)
        source_tile = origin(tile, index // chans, tiles)
        source_chan = origin(chan, index % chans, chans)
        return pltpu.make_async_copy(
            blocks[shift * tiles * chans + index].at[segment],
            features.at[frame, source_chan, source_tile],
            arrived.at[shift, index],
        )

    def every_copy(segment):
        for shift in range(frames):
            for index in range(tiles * chans):
                yield copy_in(segment, shift, index)

    def weight_copies():
        for side in range(chans):
            place = pl.multiple_of(origin(chan, side, chans) * part, part)
            for row in range(TAPS):
                yield pltpu.make_async_copy(
                    sides[side].at[pl.ds(row * part, part)],
                    weights.at[pl.ds(row * channels + place, part)],
                    fetched.at[side, row],
                )

    def bias_of(index):
        block = weights[:channels, starts[-1] : starts[-1] + LANES].astype(jnp.float32)
        lane = lax.broadcasted_iota(jnp.int32, block.shape, 1)
        mine = (lane >= PIECES * index) & (lane < PIECES * (index + 1))
        column = jnp.sum(jnp.where(mine, block, 0.0), axis=1, keepdims=True)
        return jnp.broadcast_to(column, (channels, cols))

    def convolve(inputs, index, emit):
        low = starts[index]
        matrix = weights[:, low : low + TAPS * channels * len(inputs)]
        bias = bias_of(index)

        def step(block, carried):
            above, here = carried
            slabs = [
                jnp.concatenate([taps(load(block, row)) for load in inputs], axis=0)
                for row in range(depth)
            ]
            partial = jnp.dot(
                matrix, jnp.concatenate(slabs, axis=1), preferred_element_type=jnp.float32
            )
            for row in range(depth):
                one = partial[:, row * cols : (row + 1) * cols]
                emit(block * depth + row, above + one[2 * channels :])
                above = here + one[channels : 2 * channels]
                here = bias + one[:channels]
            return above, here

        unroll = UNROLL if tiles % UNROLL == 0 else 1
        above, _ = lax.fori_loop(0, tiles, step, (bias, bias), unroll=unroll)
        emit(rows, above)

    def stored(ref):
        return lambda block, row: ref[block * depth + row + 1]

    def displaced(held, field):
        def load(block, row):
            down = table[block, field]
            right = table[block, field + 1]
            return moved(held[top + block * depth + row + down], right)

        return load

    for copy in weight_copies():
        copy.start()
    for segment in range(count):
        for copy in every_copy(segment):
            copy.start()
        if segment == 0:
            for index in range(kept):
                history[index, :top] = jnp.zeros((top, channels, cols), jnp.bfloat16)
                history[index, top + rows :] = jnp.zeros((depth, channels, cols), jnp.bfloat16)
            for copy in weight_copies():
                copy.wait()
        for copy in every_copy(segment):
            copy.wait()
        for block in range(tiles):
            tail = features[0, 0, block, part * depth :].astype(jnp.float32).astype(jnp.int32)
            numbers[block : block + 1, :] = tail[:1]
        to_table = pltpu.make_async_copy(numbers, table, counted)
        to_table.start()
        for frame in range(frames):
            def load_own(block, row, frame=frame):
                pieces = [
                    features[frame, side, block, row * part : (row + 1) * part]
                    for side in range(chans)
                ]
                return jnp.concatenate(pieces, axis=0)

            inputs = [load_own]
            for back, field in ((1, 2 * frame), (2, 2 * (frames + frame))):
                if frame >= back:
                    inputs.append(displaced(history.at[(frame - back) % kept], field))
            if frame == min(1, frames - 1):
                to_table.wait()
            new = history.at[frame % kept]

            def emit_join(slot, total):
                joined[slot] = jnp.where(total > 0, total, 0.1 * total).astype(jnp.bfloat16)

            def emit_inner(slot, total):
                inner[slot] = jnp.maximum(total, 0.0).astype(jnp.bfloat16)

            def emit_second(slot, total, new=new):
                state = joined[slot].astype(jnp.float32) + total
                new[top - 1 + slot] = state.astype(jnp.bfloat16)

            convolve(inputs, 0, emit_join)
            convolve([stored(joined)], 1, emit_inner)
            convolve([stored(inner)], 2, emit_second)
            new[top - 1] = jnp.zeros((channels, cols), jnp.bfloat16)

            @pl.when(frame_here == frame)
            def _(segment=segment, new=new):
                for turn in range(groups):
                    target = partner(tile // span, turn, groups) * span + lax.rem(tile, span)
                    for row in range(depth):
                        value = new[
                            top + target * depth + row, pl.ds(pl.multiple_of(chan * part, part), part)
                        ]
                        stage[turn, pl.ds(row, part, stride=depth), :] = value.astype(jnp.float32)
                    whole = stage[turn].reshape(part, depth, cols)
                    outs[turn][segment] = whole.astype(jnp.bfloat16)


def shards(lr_feats, flow_prev, flow_second, w_join, b_join, w_first, b_first, w_second, b_second):
    segments, _, part, depth, cols = lr_feats.shape
    frames, tiles, chans = (lax.axis_size(name) for name in ("frames", "tiles", "chan"))
    span, groups, count = split_of(segments, tiles)
    channels = part * chans
    rows = tiles * depth
    kept = min(frames, 3)
    tall = part * depth + TAIL
    slots = tiles * count

    flows = [flow.transpose(1, 2, 3, 0) for flow in (flow_prev, flow_second)]
    packed = call(
        pack,
        in_hbm(lr_feats, *flows),
        [jax.ShapeDtypeStruct((count, tall, cols), jnp.bfloat16)] * tiles,
        [
            pltpu.VMEM((slots, part, depth, cols), jnp.bfloat16),
            pltpu.SMEM(flows[0].shape, jnp.int32),
            pltpu.SMEM(flows[1].shape, jnp.int32),
            pltpu.VMEM((slots, part * depth, cols), jnp.float32),
            pltpu.SemaphoreType.DMA((slots + 2,)),
        ],
        [HBM] * 3,
        [VMEM] * tiles,
    )

    widths = (w_join.shape[2], w_first.shape[3], w_second.shape[3])
    wide = starts_of(widths)[-1] + LANES
    own = {0: packed[0]}
    for shift in ranked(tiles):
        own[shift] = hop(packed[shift], "tiles", shift)
    params = (w_join, w_first[0], w_second[0], b_join[None], b_first, b_second)
    arranged = call(
        functools.partial(arrange, widths),
        in_hbm(*params),
        jax.ShapeDtypeStruct((TAPS * part, wide), jnp.bfloat16),
        [pltpu.VMEM(item.shape, item.dtype) for item in params]
        + [pltpu.SemaphoreType.DMA((len(params),))],
        [HBM] * len(params),
        VMEM,
    )
    sides = [hop(arranged, "chan", side) for side in range(chans)]

    blocks = []
    for turn in range(frames):
        for shift in range(tiles):
            block = hop(own[shift], "frames", turn)
            blocks += [hop(block, "chan", side) for side in range(chans)]

    outs = call(
        functools.partial(recurrence, (frames, tiles, chans, segments, part, depth, cols), widths),
        (*sides, *blocks),
        [jax.ShapeDtypeStruct((count, part, depth, cols), jnp.bfloat16)] * groups,
        [
            pltpu.VMEM((TAPS * channels, wide), jnp.bfloat16),
            pltpu.VMEM((tiles, cols), jnp.int32),
            pltpu.SMEM((tiles, cols), jnp.int32),
            pltpu.VMEM((frames, chans, tiles, tall, cols), jnp.bfloat16),
            pltpu.VMEM((rows + 1, channels, cols), jnp.bfloat16),
            pltpu.VMEM((rows + 1, channels, cols), jnp.bfloat16),
            pltpu.VMEM((kept, rows + 2 * depth + 1, channels, cols), jnp.bfloat16),
            pltpu.VMEM((groups, part * depth, cols), jnp.float32),
            pltpu.SemaphoreType.DMA((chans, TAPS)),
            pltpu.SemaphoreType.DMA((frames, tiles * chans)),
            pltpu.SemaphoreType.DMA(()),
        ],
        [VMEM] * (chans + len(blocks)),
        [VMEM] * groups,
    )
    returned = {0: outs[0]}
    for turn in ranked(groups):
        returned[turn] = hop(outs[turn], "tiles", turn, span)
    return call(
        unpack,
        tuple(returned[turn] for turn in range(groups)),
        jax.ShapeDtypeStruct(lr_feats.shape, lr_feats.dtype),
        [pltpu.SemaphoreType.DMA((segments,))],
        [VMEM] * groups,
        HBM,
    )


def solution(mesh):
    in_specs = (
        P("clips", "frames", "chan", "tiles", None),
        P("clips", None, "tiles", None),
        P("clips", None, "tiles", None),
        P(None, "chan", None),
        P("chan"),
        P(None, None, "chan", None),
        P(None, "chan"),
        P(None, None, "chan", None),
        P(None, "chan"),
    )
    out_specs = P("clips", "frames", "chan", "tiles", None)
    return jax.shard_map(
        shards,
        mesh=mesh,
        in_specs=in_specs,
        out_specs=out_specs,
        check_vma=False,
    )
```

profile of v0, /device:TPU:0, one launch (start us, length us, event | category | flops | bytes accessed | tf_op | source)
XLA Modules:
  0.0 38.7 jit_solution(17369815376319721777)
XLA Ops:
  0.0 1.1 %shard_map.92 = (bf16[1,264,128]{2,1,0:T(8,128)(2,1)S(1)}, bf16[1,264,128]{2,1,0:T(8,128)(2,1)S(1)}, bf16[1,264,128]{2,1,0:T(8,128)(2,1)S(1)}, bf16[1,264,128]{2,1,0:T(8,128)(2,1)S(1)}) custom-call(bf16[4,1,32,8,128]{4,3,2,1,0:T(8,128)(2,1)} %lr_feats.1, s32[2,1,2,4]{3,2,1,0:T(2,128)} %bitcast.7, s32[2,1,2,4]{3,2,1,0:T(2,128)} %bitcast.8), custom_call_target="tpu_custom_call" | custom-call | tf_op jit(solution)/shard_map/pallas_call | solution.py:60
  1.1 3.1 %collective-permute-start.2 = (bf16[1,264,128]{2,1,0:T(8,128)(2,1)S(1)}, bf16[1,264,128]{2,1,0:T(8,128)(2,1)S(1)}, u32[]{:S(2)}, u32[]{:S(2)}) collective-permute-start(bf16[1,264,128]{2,1,0:T(8,128)(2,1)S(1)} %get-tuple-element.14), channel_id=1, source_target_pairs={{0,4},{4,8},{8,12},{12,0},{1,5},{5,9},{9,13},{13,1},{2,6},{6,10},{... | collective-permute-start | bytes 202760 | tf_op jit(solution)/shard_map/ppermute | solution.py:39
  4.2 2.6 %collective-permute-start.4 = (bf16[1,264,128]{2,1,0:T(8,128)(2,1)S(1)}, bf16[1,264,128]{2,1,0:T(8,128)(2,1)S(1)}, u32[]{:S(2)}, u32[]{:S(2)}) collective-permute-start(bf16[1,264,128]{2,1,0:T(8,128)(2,1)S(1)} %get-tuple-element.15), channel_id=1, source_target_pairs={{0,8},{4,12},{8,0},{12,4},{1,9},{5,13},{9,1},{13,5},{2,10},{6,14},... | collective-permute-start | bytes 202760 | tf_op jit(solution)/shard_map/ppermute | solution.py:39
  6.8 1.3 %collective-permute-start.6 = (bf16[1,264,128]{2,1,0:T(8,128)(2,1)S(1)}, bf16[1,264,128]{2,1,0:T(8,128)(2,1)S(1)}, u32[]{:S(2)}, u32[]{:S(2)}) collective-permute-start(bf16[1,264,128]{2,1,0:T(8,128)(2,1)S(1)} %get-tuple-element.16), channel_id=1, source_target_pairs={{0,12},{4,0},{8,4},{12,8},{1,13},{5,1},{9,5},{13,9},{2,14},{6,2},{... | collective-permute-start | bytes 202760 | tf_op jit(solution)/shard_map/ppermute | solution.py:39
  8.1 1.2 %shard_map.91.refs_0_ = bf16[96,1280]{1,0:T(8,128)(2,1)S(1)} custom-call(bf16[9,32,192]{2,1,0:T(8,128)(2,1)} %refs_0_.1, bf16[9,32,64]{2,1,0:T(8,128)(2,1)} %bitcast.5, bf16[9,32,64]{2,1,0:T(8,128)(2,1)} %bitcast.6, f32[1,32]{1,0:T(1,128)} %bitcast.9, f32[1,32]{1,0:T(1,128)} %refs_4_.1, f32[1,32]{1,0:T(1,128)} %refs_5_.1), custom_call_target="tpu_custom_call" | custom-call | tf_op jit(solution)/shard_map/pallas_call | solution.py:60
  9.3 0.1 collective-permute-start
  9.4 1.6 %collective-permute-start.8 = (bf16[1,264,128]{2,1,0:T(8,128)(2,1)S(1)}, bf16[1,264,128]{2,1,0:T(8,128)(2,1)S(1)}, u32[]{:S(2)}, u32[]{:S(2)}) collective-permute-start(bf16[1,264,128]{2,1,0:T(8,128)(2,1)S(1)} %get-tuple-element.13.refs_2_), channel_id=1, source_target_pairs={{0,2},{2,0},{1,3},{3,1},{4,6},{6,4},{5,7},{7,5},{8,10},{10,8},{9,1... | collective-permute-start | bytes 202760 | tf_op jit(solution)/shard_map/ppermute | solution.py:39
  11.0 0.0 collective-permute-done.2.refs_4_
  11.0 0.2 collective-permute-start.1
  11.1 0.2 collective-permute-done.4.refs_6_
  11.4 1.7 %collective-permute-start.10 = (bf16[1,264,128]{2,1,0:T(8,128)(2,1)S(1)}, bf16[1,264,128]{2,1,0:T(8,128)(2,1)S(1)}, u32[]{:S(2)}, u32[]{:S(2)}) collective-permute-start(bf16[1,264,128]{2,1,0:T(8,128)(2,1)S(1)} %collective-permute-done.2.refs_4_), channel_id=1, source_target_pairs={{0,2},{2,0},{1,3},{3,1},{4,6},{6,4},{5,7},{7,5},{8,10},{10,8},{9,1... | collective-permute-start | bytes 202760 | tf_op jit(solution)/shard_map/ppermute | solution.py:39
  13.1 0.0 collective-permute-done.6.refs_8_
  13.1 0.0 collective-permute-start.3
  13.1 0.9 %collective-permute-done.8.refs_10_ = bf16[1,264,128]{2,1,0:T(8,128)(2,1)S(1)} collective-permute-done((bf16[1,264,128]{2,1,0:T(8,128)(2,1)S(1)}, bf16[1,264,128]{2,1,0:T(8,128)(2,1)S(1)}, u32[]{:S(2)}, u32[]{:S(2)}) %collective-permute-start.8) | collective-permute-done | bytes 67616 | tf_op jit(solution)/shard_map/ppermute | solution.py:39
  14.0 1.8 %collective-permute-start.12 = (bf16[1,264,128]{2,1,0:T(8,128)(2,1)S(1)}, bf16[1,264,128]{2,1,0:T(8,128)(2,1)S(1)}, u32[]{:S(2)}, u32[]{:S(2)}) collective-permute-start(bf16[1,264,128]{2,1,0:T(8,128)(2,1)S(1)} %collective-permute-done.4.refs_6_), channel_id=1, source_target_pairs={{0,2},{2,0},{1,3},{3,1},{4,6},{6,4},{5,7},{7,5},{8,10},{10,8},{9,1... | collective-permute-start | bytes 202760 | tf_op jit(solution)/shard_map/ppermute | solution.py:39
  15.8 0.0 collective-permute-done.1.refs_3_
  15.8 0.0 collective-permute-start.5
  15.8 0.0 collective-permute-done.10.refs_12_
  15.8 1.5 %collective-permute-start.14 = (bf16[1,264,128]{2,1,0:T(8,128)(2,1)S(1)}, bf16[1,264,128]{2,1,0:T(8,128)(2,1)S(1)}, u32[]{:S(2)}, u32[]{:S(2)}) collective-permute-start(bf16[1,264,128]{2,1,0:T(8,128)(2,1)S(1)} %collective-permute-done.6.refs_8_), channel_id=1, source_target_pairs={{0,2},{2,0},{1,3},{3,1},{4,6},{6,4},{5,7},{7,5},{8,10},{10,8},{9,1... | collective-permute-start | bytes 202760 | tf_op jit(solution)/shard_map/ppermute | solution.py:39
  17.4 0.0 collective-permute-done.3.refs_5_
  17.4 0.0 collective-permute-start.7
  17.4 0.9 %collective-permute-done.12.refs_14_ = bf16[1,264,128]{2,1,0:T(8,128)(2,1)S(1)} collective-permute-done((bf16[1,264,128]{2,1,0:T(8,128)(2,1)S(1)}, bf16[1,264,128]{2,1,0:T(8,128)(2,1)S(1)}, u32[]{:S(2)}, u32[]{:S(2)}) %collective-permute-start.12) | collective-permute-done | bytes 67616 | tf_op jit(solution)/shard_map/ppermute | solution.py:39
  18.3 0.0 collective-permute-start.9
  18.3 0.0 collective-permute-done.5.refs_7_
  18.3 0.5 %collective-permute-start.11 = (bf16[1,264,128]{2,1,0:T(8,128)(2,1)S(1)}, bf16[1,264,128]{2,1,0:T(8,128)(2,1)S(1)}, u32[]{:S(2)}, u32[]{:S(2)}) collective-permute-start(bf16[1,264,128]{2,1,0:T(8,128)(2,1)S(1)} %collective-permute-done.10.refs_12_), channel_id=1, source_target_pairs={{0,1},{1,0},{2,3},{3,2},{4,5},{5,4},{6,7},{7,6},{8,9},{9,8},{10,11... | collective-permute-start | bytes 202760 | tf_op jit(solution)/shard_map/ppermute | solution.py:39
  18.8 1.6 %collective-permute-done.14.refs_16_ = bf16[1,264,128]{2,1,0:T(8,128)(2,1)S(1)} collective-permute-done((bf16[1,264,128]{2,1,0:T(8,128)(2,1)S(1)}, bf16[1,264,128]{2,1,0:T(8,128)(2,1)S(1)}, u32[]{:S(2)}, u32[]{:S(2)}) %collective-permute-start.14) | collective-permute-done | bytes 67616 | tf_op jit(solution)/shard_map/ppermute | solution.py:39
  20.4 0.0 collective-permute-start.13
  20.4 0.0 collective-permute-done.7.refs_9_
  20.4 0.5 %collective-permute-start.15 = (bf16[1,264,128]{2,1,0:T(8,128)(2,1)S(1)}, bf16[1,264,128]{2,1,0:T(8,128)(2,1)S(1)}, u32[]{:S(2)}, u32[]{:S(2)}) collective-permute-start(bf16[1,264,128]{2,1,0:T(8,128)(2,1)S(1)} %collective-permute-done.14.refs_16_), channel_id=1, source_target_pairs={{0,1},{1,0},{2,3},{3,2},{4,5},{5,4},{6,7},{7,6},{8,9},{9,8},{10,11... | collective-permute-start | bytes 202760 | tf_op jit(solution)/shard_map/ppermute | solution.py:39
  20.9 0.0 collective-permute-done.9.refs_11_
  20.9 0.0 collective-permute-done.11.refs_13_
  20.9 0.7 %collective-permute-done.13.refs_15_ = bf16[1,264,128]{2,1,0:T(8,128)(2,1)S(1)} collective-permute-done((bf16[1,264,128]{2,1,0:T(8,128)(2,1)S(1)}, bf16[1,264,128]{2,1,0:T(8,128)(2,1)S(1)}, u32[]{:S(2)}, u32[]{:S(2)}) %collective-permute-start.13) | collective-permute-done | bytes 67616 | tf_op jit(solution)/shard_map/ppermute | solution.py:39
  21.6 0.2 collective-permute-done.15.refs_17_
  21.8 0.0 collective-permute-done.refs_1_
  21.8 7.1 %shard_map.93 = (bf16[1,32,8,128]{3,2,1,0:T(8,128)(2,1)S(1)}, bf16[1,32,8,128]{3,2,1,0:T(8,128)(2,1)S(1)}, bf16[1,32,8,128]{3,2,1,0:T(8,128)(2,1)S(1)}, bf16[1,32,8,128]{3,2,1,0:T(8,128)(2,1)S(1)}) custom-call(bf16[96,1280]{1,0:T(8,128)(2,1)S(1)} %shard_map.91.refs_0_, bf16[96,1280]{1,0:T(8,128)(2,1)S(1)} %collective-permute-done.refs_1_, ...), custom_call_target="tpu_custom_call" | custom-call | tf_op jit(solution)/shard_map/pallas_call | solution.py:60
  28.9 0.9 %collective-permute-start.16 = (bf16[1,32,8,128]{3,2,1,0:T(8,128)(2,1)S(1)}, bf16[1,32,8,128]{3,2,1,0:T(8,128)(2,1)S(1)}, u32[]{:S(2)}, u32[]{:S(2)}) collective-permute-start(bf16[1,32,8,128]{3,2,1,0:T(8,128)(2,1)S(1)} %get-tuple-element.18), channel_id=1, source_target_pairs={{0,4},{4,8},{8,12},{12,0},{1,5},{5,9},{9,13},{13,1},{2,6},{6,10},{... | collective-permute-start | bytes 196616 | tf_op jit(solution)/shard_map/ppermute | solution.py:39
  29.8 2.7 %collective-permute-start.17 = (bf16[1,32,8,128]{3,2,1,0:T(8,128)(2,1)S(1)}, bf16[1,32,8,128]{3,2,1,0:T(8,128)(2,1)S(1)}, u32[]{:S(2)}, u32[]{:S(2)}) collective-permute-start(bf16[1,32,8,128]{3,2,1,0:T(8,128)(2,1)S(1)} %get-tuple-element.19), channel_id=1, source_target_pairs={{0,8},{4,12},{8,0},{12,4},{1,9},{5,13},{9,1},{13,5},{2,10},{6,14},... | collective-permute-start | bytes 196616 | tf_op jit(solution)/shard_map/ppermute | solution.py:39
  32.5 0.3 collective-permute-start.18
  32.8 3.0 %collective-permute-done.16.refs_1_ = bf16[1,32,8,128]{3,2,1,0:T(8,128)(2,1)S(1)} collective-permute-done((bf16[1,32,8,128]{3,2,1,0:T(8,128)(2,1)S(1)}, bf16[1,32,8,128]{3,2,1,0:T(8,128)(2,1)S(1)}, u32[]{:S(2)}, u32[]{:S(2)}) %collective-permute-start.16) | collective-permute-done | bytes 65568 | tf_op jit(solution)/shard_map/ppermute | solution.py:39
  35.8 2.2 %collective-permute-done.17.refs_2_ = bf16[1,32,8,128]{3,2,1,0:T(8,128)(2,1)S(1)} collective-permute-done((bf16[1,32,8,128]{3,2,1,0:T(8,128)(2,1)S(1)}, bf16[1,32,8,128]{3,2,1,0:T(8,128)(2,1)S(1)}, u32[]{:S(2)}, u32[]{:S(2)}) %collective-permute-start.17) | collective-permute-done | bytes 65568 | tf_op jit(solution)/shard_map/ppermute | solution.py:39
  38.0 0.0 collective-permute-done.18.refs_3_
  38.0 0.7 %shard_map.94 = bf16[4,1,32,8,128]{4,3,2,1,0:T(8,128)(2,1)} custom-call(bf16[1,32,8,128]{3,2,1,0:T(8,128)(2,1)S(1)} %get-tuple-element.17.refs_0_, bf16[1,32,8,128]{3,2,1,0:T(8,128)(2,1)S(1)} %collective-permute-done.16.refs_1_, bf16[1,32,8,128]{3,2,1,0:T(8,128)(2,1)S(1)} %collective-permute-done.17.refs_2_, ...), custom_call_target="tpu_custom_call" | custom-call | tf_op jit(solution)/shard_map/pallas_call | solution.py:60
Async XLA Ops:
  1.1 9.9 %collective-permute-start.2 = (bf16[1,264,128]{2,1,0:T(8,128)(2,1)S(1)}, bf16[1,264,128]{2,1,0:T(8,128)(2,1)S(1)}, u32[]{:S(2)}, u32[]{:S(2)}) collective-permute-start(bf16[1,264,128]{2,1,0:T(8,128)(2,1)S(1)} %get-tuple-element.14), channel_id=1, source_target_pairs={{0,4},{4,8},{8,12},{12,0},{1,5},{5,9},{9,13},{13,1},{2,6},{6,10},{... | collective-permute-start | bytes 202760 | tf_op jit(solution)/shard_map/ppermute | solution.py:39
  4.2 7.2 %collective-permute-start.4 = (bf16[1,264,128]{2,1,0:T(8,128)(2,1)S(1)}, bf16[1,264,128]{2,1,0:T(8,128)(2,1)S(1)}, u32[]{:S(2)}, u32[]{:S(2)}) collective-permute-start(bf16[1,264,128]{2,1,0:T(8,128)(2,1)S(1)} %get-tuple-element.15), channel_id=1, source_target_pairs={{0,8},{4,12},{8,0},{12,4},{1,9},{5,13},{9,1},{13,5},{2,10},{6,14},... | collective-permute-start | bytes 202760 | tf_op jit(solution)/shard_map/ppermute | solution.py:39
  6.8 6.3 %collective-permute-start.6 = (bf16[1,264,128]{2,1,0:T(8,128)(2,1)S(1)}, bf16[1,264,128]{2,1,0:T(8,128)(2,1)S(1)}, u32[]{:S(2)}, u32[]{:S(2)}) collective-permute-start(bf16[1,264,128]{2,1,0:T(8,128)(2,1)S(1)} %get-tuple-element.16), channel_id=1, source_target_pairs={{0,12},{4,0},{8,4},{12,8},{1,13},{5,1},{9,5},{13,9},{2,14},{6,2},{... | collective-permute-start | bytes 202760 | tf_op jit(solution)/shard_map/ppermute | solution.py:39
  9.3 12.4 %collective-permute-start = (bf16[96,1280]{1,0:T(8,128)(2,1)S(1)}, bf16[96,1280]{1,0:T(8,128)(2,1)S(1)}, u32[]{:S(2)}, u32[]{:S(2)}) collective-permute-start(bf16[96,1280]{1,0:T(8,128)(2,1)S(1)} %shard_map.91.refs_0_), channel_id=1, source_target_pairs={{0,1},{1,0},{2,3},{3,2},{4,5},{5,4},{6,7},{7,6},{8,9},{9,8},{10,11... | collective-permute-start | bytes 737288 | tf_op jit(solution)/shard_map/ppermute | solution.py:39
  9.4 4.5 %collective-permute-start.8 = (bf16[1,264,128]{2,1,0:T(8,128)(2,1)S(1)}, bf16[1,264,128]{2,1,0:T(8,128)(2,1)S(1)}, u32[]{:S(2)}, u32[]{:S(2)}) collective-permute-start(bf16[1,264,128]{2,1,0:T(8,128)(2,1)S(1)} %get-tuple-element.13.refs_2_), channel_id=1, source_target_pairs={{0,2},{2,0},{1,3},{3,1},{4,6},{6,4},{5,7},{7,5},{8,10},{10,8},{9,1... | collective-permute-start | bytes 202760 | tf_op jit(solution)/shard_map/ppermute | solution.py:39
  11.0 4.8 %collective-permute-start.1 = (bf16[1,264,128]{2,1,0:T(8,128)(2,1)S(1)}, bf16[1,264,128]{2,1,0:T(8,128)(2,1)S(1)}, u32[]{:S(2)}, u32[]{:S(2)}) collective-permute-start(bf16[1,264,128]{2,1,0:T(8,128)(2,1)S(1)} %get-tuple-element.13.refs_2_), channel_id=1, source_target_pairs={{0,1},{1,0},{2,3},{3,2},{4,5},{5,4},{6,7},{7,6},{8,9},{9,8},{10,11... | collective-permute-start | bytes 202760 | tf_op jit(solution)/shard_map/ppermute | solution.py:39
  11.4 4.4 %collective-permute-start.10 = (bf16[1,264,128]{2,1,0:T(8,128)(2,1)S(1)}, bf16[1,264,128]{2,1,0:T(8,128)(2,1)S(1)}, u32[]{:S(2)}, u32[]{:S(2)}) collective-permute-start(bf16[1,264,128]{2,1,0:T(8,128)(2,1)S(1)} %collective-permute-done.2.refs_4_), channel_id=1, source_target_pairs={{0,2},{2,0},{1,3},{3,1},{4,6},{6,4},{5,7},{7,5},{8,10},{10,8},{9,1... | collective-permute-start | bytes 202760 | tf_op jit(solution)/shard_map/ppermute | solution.py:39
  13.1 4.3 %collective-permute-start.3 = (bf16[1,264,128]{2,1,0:T(8,128)(2,1)S(1)}, bf16[1,264,128]{2,1,0:T(8,128)(2,1)S(1)}, u32[]{:S(2)}, u32[]{:S(2)}) collective-permute-start(bf16[1,264,128]{2,1,0:T(8,128)(2,1)S(1)} %collective-permute-done.2.refs_4_), channel_id=1, source_target_pairs={{0,1},{1,0},{2,3},{3,2},{4,5},{5,4},{6,7},{7,6},{8,9},{9,8},{10,11... | collective-permute-start | bytes 202760 | tf_op jit(solution)/shard_map/ppermute | solution.py:39
  14.0 4.3 %collective-permute-start.12 = (bf16[1,264,128]{2,1,0:T(8,128)(2,1)S(1)}, bf16[1,264,128]{2,1,0:T(8,128)(2,1)S(1)}, u32[]{:S(2)}, u32[]{:S(2)}) collective-permute-start(bf16[1,264,128]{2,1,0:T(8,128)(2,1)S(1)} %collective-permute-done.4.refs_6_), channel_id=1, source_target_pairs={{0,2},{2,0},{1,3},{3,1},{4,6},{6,4},{5,7},{7,5},{8,10},{10,8},{9,1... | collective-permute-start | bytes 202760 | tf_op jit(solution)/shard_map/ppermute | solution.py:39
  15.8 2.4 %collective-permute-start.5 = (bf16[1,264,128]{2,1,0:T(8,128)(2,1)S(1)}, bf16[1,264,128]{2,1,0:T(8,128)(2,1)S(1)}, u32[]{:S(2)}, u32[]{:S(2)}) collective-permute-start(bf16[1,264,128]{2,1,0:T(8,128)(2,1)S(1)} %collective-permute-done.4.refs_6_), channel_id=1, source_target_pairs={{0,1},{1,0},{2,3},{3,2},{4,5},{5,4},{6,7},{7,6},{8,9},{9,8},{10,11... | collective-permute-start | bytes 202760 | tf_op jit(solution)/shard_map/ppermute | solution.py:39
  15.8 4.5 %collective-permute-start.14 = (bf16[1,264,128]{2,1,0:T(8,128)(2,1)S(1)}, bf16[1,264,128]{2,1,0:T(8,128)(2,1)S(1)}, u32[]{:S(2)}, u32[]{:S(2)}) collective-permute-start(bf16[1,264,128]{2,1,0:T(8,128)(2,1)S(1)} %collective-permute-done.6.refs_8_), channel_id=1, source_target_pairs={{0,2},{2,0},{1,3},{3,1},{4,6},{6,4},{5,7},{7,5},{8,10},{10,8},{9,1... | collective-permute-start | bytes 202760 | tf_op jit(solution)/shard_map/ppermute | solution.py:39
  17.4 3.0 %collective-permute-start.7 = (bf16[1,264,128]{2,1,0:T(8,128)(2,1)S(1)}, bf16[1,264,128]{2,1,0:T(8,128)(2,1)S(1)}, u32[]{:S(2)}, u32[]{:S(2)}) collective-permute-start(bf16[1,264,128]{2,1,0:T(8,128)(2,1)S(1)} %collective-permute-done.6.refs_8_), channel_id=1, source_target_pairs={{0,1},{1,0},{2,3},{3,2},{4,5},{5,4},{6,7},{7,6},{8,9},{9,8},{10,11... | collective-permute-start | bytes 202760 | tf_op jit(solution)/shard_map/ppermute | solution.py:39
  18.3 2.6 %collective-permute-start.9 = (bf16[1,264,128]{2,1,0:T(8,128)(2,1)S(1)}, bf16[1,264,128]{2,1,0:T(8,128)(2,1)S(1)}, u32[]{:S(2)}, u32[]{:S(2)}) collective-permute-start(bf16[1,264,128]{2,1,0:T(8,128)(2,1)S(1)} %collective-permute-done.8.refs_10_), channel_id=1, source_target_pairs={{0,1},{1,0},{2,3},{3,2},{4,5},{5,4},{6,7},{7,6},{8,9},{9,8},{10,11... | collective-permute-start | bytes 202760 | tf_op jit(solution)/shard_map/ppermute | solution.py:39
  18.3 2.6 %collective-permute-start.11 = (bf16[1,264,128]{2,1,0:T(8,128)(2,1)S(1)}, bf16[1,264,128]{2,1,0:T(8,128)(2,1)S(1)}, u32[]{:S(2)}, u32[]{:S(2)}) collective-permute-start(bf16[1,264,128]{2,1,0:T(8,128)(2,1)S(1)} %collective-permute-done.10.refs_12_), channel_id=1, source_target_pairs={{0,1},{1,0},{2,3},{3,2},{4,5},{5,4},{6,7},{7,6},{8,9},{9,8},{10,11... | collective-permute-start | bytes 202760 | tf_op jit(solution)/shard_map/ppermute | solution.py:39
  20.4 1.3 %collective-permute-start.13 = (bf16[1,264,128]{2,1,0:T(8,128)(2,1)S(1)}, bf16[1,264,128]{2,1,0:T(8,128)(2,1)S(1)}, u32[]{:S(2)}, u32[]{:S(2)}) collective-permute-start(bf16[1,264,128]{2,1,0:T(8,128)(2,1)S(1)} %collective-permute-done.12.refs_14_), channel_id=1, source_target_pairs={{0,1},{1,0},{2,3},{3,2},{4,5},{5,4},{6,7},{7,6},{8,9},{9,8},{10,11... | collective-permute-start | bytes 202760 | tf_op jit(solution)/shard_map/ppermute | solution.py:39
  20.4 1.4 %collective-permute-start.15 = (bf16[1,264,128]{2,1,0:T(8,128)(2,1)S(1)}, bf16[1,264,128]{2,1,0:T(8,128)(2,1)S(1)}, u32[]{:S(2)}, u32[]{:S(2)}) collective-permute-start(bf16[1,264,128]{2,1,0:T(8,128)(2,1)S(1)} %collective-permute-done.14.refs_16_), channel_id=1, source_target_pairs={{0,1},{1,0},{2,3},{3,2},{4,5},{5,4},{6,7},{7,6},{8,9},{9,8},{10,11... | collective-permute-start | bytes 202760 | tf_op jit(solution)/shard_map/ppermute | solution.py:39
  28.9 6.9 %collective-permute-start.16 = (bf16[1,32,8,128]{3,2,1,0:T(8,128)(2,1)S(1)}, bf16[1,32,8,128]{3,2,1,0:T(8,128)(2,1)S(1)}, u32[]{:S(2)}, u32[]{:S(2)}) collective-permute-start(bf16[1,32,8,128]{3,2,1,0:T(8,128)(2,1)S(1)} %get-tuple-element.18), channel_id=1, source_target_pairs={{0,4},{4,8},{8,12},{12,0},{1,5},{5,9},{9,13},{13,1},{2,6},{6,10},{... | collective-permute-start | bytes 196616 | tf_op jit(solution)/shard_map/ppermute | solution.py:39
  29.8 8.2 %collective-permute-start.17 = (bf16[1,32,8,128]{3,2,1,0:T(8,128)(2,1)S(1)}, bf16[1,32,8,128]{3,2,1,0:T(8,128)(2,1)S(1)}, u32[]{:S(2)}, u32[]{:S(2)}) collective-permute-start(bf16[1,32,8,128]{3,2,1,0:T(8,128)(2,1)S(1)} %get-tuple-element.19), channel_id=1, source_target_pairs={{0,8},{4,12},{8,0},{12,4},{1,9},{5,13},{9,1},{13,5},{2,10},{6,14},... | collective-permute-start | bytes 196616 | tf_op jit(solution)/shard_map/ppermute | solution.py:39
  32.5 5.5 %collective-permute-start.18 = (bf16[1,32,8,128]{3,2,1,0:T(8,128)(2,1)S(1)}, bf16[1,32,8,128]{3,2,1,0:T(8,128)(2,1)S(1)}, u32[]{:S(2)}, u32[]{:S(2)}) collective-permute-start(bf16[1,32,8,128]{3,2,1,0:T(8,128)(2,1)S(1)} %get-tuple-element.20), channel_id=1, source_target_pairs={{0,12},{4,0},{8,4},{12,8},{1,13},{5,1},{9,5},{13,9},{2,14},{6,2},{... | collective-permute-start | bytes 196616 | tf_op jit(solution)/shard_map/ppermute | solution.py:39
where the time goes:
time: 38.9 us; the launch traced here: 38.7 us
  starting transfers between devices  18.8 us (48%)
  Pallas kernels  10.1 us (26%)
  waiting for transfers between devices  9.74 us (25%)
    ppermute x19, starting transfers between devices, hop(): return lax.ppermute(array, axis, pairs)  18.8 us
    pallas_call x4, Pallas kernels, call(): pl.pallas_call(kernel, out_shape=out_shape, in_specs=in_specs, out_specs=...  10.1 us
    ppermute x19, waiting for transfers between devices, hop(): return lax.ppermute(array, axis, pairs)  9.74 us
  transfers between devices with their start and end apart: 19, of which 8 were waited for; matrix products, arithmetic and copies ran while one was open for 0% of the time, Pallas kernels for 3%

commit v1 on v0

--- a/solution.py
+++ b/solution.py
@@ -13,7 +13,8 @@
 LANES = 128
 TAIL = 8
 PIECES = 3
-UNROLL = 4
+UNROLL = 8
+GROUP = 4
 SPARE = 4 * 2**20
 VMEM = pl.BlockSpec(memory_space=pltpu.VMEM)
 HBM = pl.BlockSpec(memory_space=pltpu.HBM)
@@ -213,8 +214,7 @@
     sides, refs = refs[:chans], refs[chans:]
     blocks, refs = refs[:n_blocks], refs[n_blocks:]
     outs, refs = refs[:groups], refs[groups:]
-    weights, numbers, table, features, joined, inner, history, stage = refs[:8]
-    fetched, arrived, counted = refs[8:]
+    weights, numbers, table, features, joined, inner, history, stage, counted = refs
     channels = part * chans
     rows = tiles * depth
     tile, frame_here, chan = (lax.axis_index(name) for name in ("tiles", "frames", "chan"))
@@ -222,30 +222,22 @@
     top = depth + 1
     starts = starts_of(widths)
 
-    def copy_in(segment, shift, index):
-        frame = origin(frame_here, shift, frames)
-        source_tile = origin(tile, index // chans, tiles)
-        source_chan = origin(chan, index % chans, chans)
-        return pltpu.make_async_copy(
-            blocks[shift * tiles * chans + index].at[segment],
-            features.at[frame, source_chan, source_tile],
-            arrived.at[shift, index],
-        )
-
-    def every_copy(segment):
+    def place_blocks(segment):
         for shift in range(frames):
+            frame = origin(frame_here, shift, frames)
             for index in range(tiles * chans):
-                yield copy_in(segment, shift, index)
-
-    def weight_copies():
+                source_tile = origin(tile, index // chans, tiles)
+                source_chan = origin(chan, index % chans, chans)
+                block = blocks[shift * tiles * chans + index]
+                features[frame, source_chan, source_tile] = block[segment]
+
+    def place_weights():
         for side in range(chans):
             place = pl.multiple_of(origin(chan, side, chans) * part, part)
             for row in range(TAPS):
-                yield pltpu.make_async_copy(
-                    sides[side].at[pl.ds(row * part, part)],
-                    weights.at[pl.ds(row * channels + place, part)],
-                    fetched.at[side, row],
-                )
+                weights[pl.ds(row * channels + place, part)] = sides[side][
+                    row * part : (row + 1) * part
+                ]
 
     def bias_of(index):
         block = weights[:channels, starts[-1] : starts[-1] + LANES].astype(jnp.float32)
@@ -259,50 +251,45 @@
         matrix = weights[:, low : low + TAPS * channels * len(inputs)]
         bias = bias_of(index)
 
-        def step(block, carried):
+        def step(turn, carried):
             above, here = carried
+            first = turn * GROUP
+            block = lax.div(first, depth)
             slabs = [
-                jnp.concatenate([taps(load(block, row)) for load in inputs], axis=0)
-                for row in range(depth)
+                jnp.concatenate([taps(load(block, first + row)) for load in inputs], axis=0)
+                for row in range(GROUP)
             ]
             partial = jnp.dot(
                 matrix, jnp.concatenate(slabs, axis=1), preferred_element_type=jnp.float32
             )
-            for row in range(depth):
+            for row in range(GROUP):
                 one = partial[:, row * cols : (row + 1) * cols]
-                emit(block * depth + row, above + one[2 * channels :])
+                emit(first + row, above + one[2 * channels :])
                 above = here + one[channels : 2 * channels]
                 here = bias + one[:channels]
             return above, here
 
-        unroll = UNROLL if tiles % UNROLL == 0 else 1
-        above, _ = lax.fori_loop(0, tiles, step, (bias, bias), unroll=unroll)
+        turns = rows // GROUP
+        above, _ = lax.fori_loop(0, turns, step, (bias, bias), unroll=math.gcd(turns, UNROLL))
         emit(rows, above)
 
     def stored(ref):
-        return lambda block, row: ref[block * depth + row + 1]
+        return lambda block, row: ref[row + 1]
 
     def displaced(held, field):
         def load(block, row):
             down = table[block, field]
             right = table[block, field + 1]
-            return moved(held[top + block * depth + row + down], right)
+            return moved(held[top + row + down], right)
 
         return load
 
-    for copy in weight_copies():
-        copy.start()
+    place_weights()
+    for index in range(kept):
+        history[index, :top] = jnp.zeros((top, channels, cols), jnp.bfloat16)
+        history[index, top + rows :] = jnp.zeros((depth, channels, cols), jnp.bfloat16)
     for segment in range(count):
-        for copy in every_copy(segment):
-            copy.start()
-        if segment == 0:
-            for index in range(kept):
-                history[index, :top] = jnp.zeros((top, channels, cols), jnp.bfloat16)
-                history[index, top + rows :] = jnp.zeros((depth, channels, cols), jnp.bfloat16)
-            for copy in weight_copies():
-                copy.wait()
-        for copy in every_copy(segment):
-            copy.wait()
+        place_blocks(segment)
         for block in range(tiles):
             tail = features[0, 0, block, part * depth :].astype(jnp.float32).astype(jnp.int32)
             numbers[block : block + 1, :] = tail[:1]
@@ -310,10 +297,8 @@
         to_table.start()
         for frame in range(frames):
             def load_own(block, row, frame=frame):
-                pieces = [
-                    features[frame, side, block, row * part : (row + 1) * part]
-                    for side in range(chans)
-                ]
+                first = pl.multiple_of(lax.rem(row, depth) * part, part)
+                pieces = [features[frame, side, block, pl.ds(first, part)] for side in range(chans)]
                 return jnp.concatenate(pieces, axis=0)
 
             inputs = [load_own]
@@ -414,8 +399,6 @@
             pltpu.VMEM((rows + 1, channels, cols), jnp.bfloat16),
             pltpu.VMEM((kept, rows + 2 * depth + 1, channels, cols), jnp.bfloat16),
             pltpu.VMEM((groups, part * depth, cols), jnp.float32),
-            pltpu.SemaphoreType.DMA((chans, TAPS)),
-            pltpu.SemaphoreType.DMA((frames, tiles * chans)),
             pltpu.SemaphoreType.DMA(()),
         ],
         [VMEM] * (chans + len(blocks)),

time: 38.9 us -> 36.4 us (0.936)
  Pallas kernels: 10.1 us -> 7.57 us
    pallas_call x4, Pallas kernels: 10.1 us -> 7.57 us  [call(): pl.pallas_call(kernel, out_shape=out_shape, in_specs=in_specs, out_specs=...]
where the time goes in v1:
time: 36.4 us; the launch traced here: 36.2 us
  starting transfers between devices  18.8 us (52%)
  waiting for transfers between devices  9.74 us (27%)
  Pallas kernels  7.57 us (21%)
    ppermute x19, starting transfers between devices, hop(): return lax.ppermute(array, axis, pairs)  18.8 us
    ppermute x19, waiting for transfers between devices, hop(): return lax.ppermute(array, axis, pairs)  9.74 us
    pallas_call x4, Pallas kernels, call(): pl.pallas_call(kernel, out_shape=out_shape, in_specs=in_specs, out_specs=...  7.57 us
  transfers between devices with their start and end apart: 19, of which 8 were waited for; matrix products, arithmetic and copies ran while one was open for 0% of the time, Pallas kernels for 3%

profile of v1, /device:TPU:0, one launch (start us, length us, event | category | flops | bytes accessed | tf_op | source)
XLA Modules:
  0.0 36.2 jit_solution(9086247209525601743)
XLA Ops:
  0.0 1.1 %shard_map.92 = (bf16[1,264,128]{2,1,0:T(8,128)(2,1)S(1)}, bf16[1,264,128]{2,1,0:T(8,128)(2,1)S(1)}, bf16[1,264,128]{2,1,0:T(8,128)(2,1)S(1)}, bf16[1,264,128]{2,1,0:T(8,128)(2,1)S(1)}) custom-call(bf16[4,1,32,8,128]{4,3,2,1,0:T(8,128)(2,1)} %lr_feats.1, s32[2,1,2,4]{3,2,1,0:T(2,128)} %bitcast.7, s32[2,1,2,4]{3,2,1,0:T(2,128)} %bitcast.8), custom_call_target="tpu_custom_call" | custom-call | tf_op jit(solution)/shard_map/pallas_call | solution.py:61
  1.1 3.1 %collective-permute-start.2 = (bf16[1,264,128]{2,1,0:T(8,128)(2,1)S(1)}, bf16[1,264,128]{2,1,0:T(8,128)(2,1)S(1)}, u32[]{:S(2)}, u32[]{:S(2)}) collective-permute-start(bf16[1,264,128]{2,1,0:T(8,128)(2,1)S(1)} %get-tuple-element.14), channel_id=1, source_target_pairs={{0,4},{4,8},{8,12},{12,0},{1,5},{5,9},{9,13},{13,1},{2,6},{6,10},{... | collective-permute-start | bytes 202760 | tf_op jit(solution)/shard_map/ppermute | solution.py:40
  4.2 2.6 %collective-permute-start.4 = (bf16[1,264,128]{2,1,0:T(8,128)(2,1)S(1)}, bf16[1,264,128]{2,1,0:T(8,128)(2,1)S(1)}, u32[]{:S(2)}, u32[]{:S(2)}) collective-permute-start(bf16[1,264,128]{2,1,0:T(8,128)(2,1)S(1)} %get-tuple-element.15), channel_id=1, source_target_pairs={{0,8},{4,12},{8,0},{12,4},{1,9},{5,13},{9,1},{13,5},{2,10},{6,14},... | collective-permute-start | bytes 202760 | tf_op jit(solution)/shard_map/ppermute | solution.py:40
  6.8 1.3 %collective-permute-start.6 = (bf16[1,264,128]{2,1,0:T(8,128)(2,1)S(1)}, bf16[1,264,128]{2,1,0:T(8,128)(2,1)S(1)}, u32[]{:S(2)}, u32[]{:S(2)}) collective-permute-start(bf16[1,264,128]{2,1,0:T(8,128)(2,1)S(1)} %get-tuple-element.16), channel_id=1, source_target_pairs={{0,12},{4,0},{8,4},{12,8},{1,13},{5,1},{9,5},{13,9},{2,14},{6,2},{... | collective-permute-start | bytes 202760 | tf_op jit(solution)/shard_map/ppermute | solution.py:40
  8.1 1.2 %shard_map.91.refs_0_ = bf16[96,1280]{1,0:T(8,128)(2,1)S(1)} custom-call(bf16[9,32,192]{2,1,0:T(8,128)(2,1)} %refs_0_.1, bf16[9,32,64]{2,1,0:T(8,128)(2,1)} %bitcast.5, bf16[9,32,64]{2,1,0:T(8,128)(2,1)} %bitcast.6, f32[1,32]{1,0:T(1,128)} %bitcast.9, f32[1,32]{1,0:T(1,128)} %refs_4_.1, f32[1,32]{1,0:T(1,128)} %refs_5_.1), custom_call_target="tpu_custom_call" | custom-call | tf_op jit(solution)/shard_map/pallas_call | solution.py:61
  9.3 0.1 collective-permute-start
  9.4 1.6 %collective-permute-start.8 = (bf16[1,264,128]{2,1,0:T(8,128)(2,1)S(1)}, bf16[1,264,128]{2,1,0:T(8,128)(2,1)S(1)}, u32[]{:S(2)}, u32[]{:S(2)}) collective-permute-start(bf16[1,264,128]{2,1,0:T(8,128)(2,1)S(1)} %get-tuple-element.13.refs_2_), channel_id=1, source_target_pairs={{0,2},{2,0},{1,3},{3,1},{4,6},{6,4},{5,7},{7,5},{8,10},{10,8},{9,1... | collective-permute-start | bytes 202760 | tf_op jit(solution)/shard_map/ppermute | solution.py:40
  11.0 0.0 collective-permute-done.2.refs_4_
  11.0 0.2 collective-permute-start.1
  11.1 0.2 collective-permute-done.4.refs_6_
  11.4 1.7 %collective-permute-start.10 = (bf16[1,264,128]{2,1,0:T(8,128)(2,1)S(1)}, bf16[1,264,128]{2,1,0:T(8,128)(2,1)S(1)}, u32[]{:S(2)}, u32[]{:S(2)}) collective-permute-start(bf16[1,264,128]{2,1,0:T(8,128)(2,1)S(1)} %collective-permute-done.2.refs_4_), channel_id=1, source_target_pairs={{0,2},{2,0},{1,3},{3,1},{4,6},{6,4},{5,7},{7,5},{8,10},{10,8},{9,1... | collective-permute-start | bytes 202760 | tf_op jit(solution)/shard_map/ppermute | solution.py:40
  13.1 0.0 collective-permute-done.6.refs_8_
  13.1 0.0 collective-permute-start.3
  13.1 0.9 %collective-permute-done.8.refs_10_ = bf16[1,264,128]{2,1,0:T(8,128)(2,1)S(1)} collective-permute-done((bf16[1,264,128]{2,1,0:T(8,128)(2,1)S(1)}, bf16[1,264,128]{2,1,0:T(8,128)(2,1)S(1)}, u32[]{:S(2)}, u32[]{:S(2)}) %collective-permute-start.8) | collective-permute-done | bytes 67616 | tf_op jit(solution)/shard_map/ppermute | solution.py:40
  14.0 1.8 %collective-permute-start.12 = (bf16[1,264,128]{2,1,0:T(8,128)(2,1)S(1)}, bf16[1,264,128]{2,1,0:T(8,128)(2,1)S(1)}, u32[]{:S(2)}, u32[]{:S(2)}) collective-permute-start(bf16[1,264,128]{2,1,0:T(8,128)(2,1)S(1)} %collective-permute-done.4.refs_6_), channel_id=1, source_target_pairs={{0,2},{2,0},{1,3},{3,1},{4,6},{6,4},{5,7},{7,5},{8,10},{10,8},{9,1... | collective-permute-start | bytes 202760 | tf_op jit(solution)/shard_map/ppermute | solution.py:40
  15.8 0.0 collective-permute-done.1.refs_3_
  15.8 0.0 collective-permute-start.5
  15.8 0.0 collective-permute-done.10.refs_12_
  15.8 1.5 %collective-permute-start.14 = (bf16[1,264,128]{2,1,0:T(8,128)(2,1)S(1)}, bf16[1,264,128]{2,1,0:T(8,128)(2,1)S(1)}, u32[]{:S(2)}, u32[]{:S(2)}) collective-permute-start(bf16[1,264,128]{2,1,0:T(8,128)(2,1)S(1)} %collective-permute-done.6.refs_8_), channel_id=1, source_target_pairs={{0,2},{2,0},{1,3},{3,1},{4,6},{6,4},{5,7},{7,5},{8,10},{10,8},{9,1... | collective-permute-start | bytes 202760 | tf_op jit(solution)/shard_map/ppermute | solution.py:40
  17.4 0.0 collective-permute-done.3.refs_5_
  17.4 0.0 collective-permute-start.7
  17.4 0.9 %collective-permute-done.12.refs_14_ = bf16[1,264,128]{2,1,0:T(8,128)(2,1)S(1)} collective-permute-done((bf16[1,264,128]{2,1,0:T(8,128)(2,1)S(1)}, bf16[1,264,128]{2,1,0:T(8,128)(2,1)S(1)}, u32[]{:S(2)}, u32[]{:S(2)}) %collective-permute-start.12) | collective-permute-done | bytes 67616 | tf_op jit(solution)/shard_map/ppermute | solution.py:40
  18.3 0.0 collective-permute-start.9
  18.3 0.0 collective-permute-done.5.refs_7_
  18.3 0.5 %collective-permute-start.11 = (bf16[1,264,128]{2,1,0:T(8,128)(2,1)S(1)}, bf16[1,264,128]{2,1,0:T(8,128)(2,1)S(1)}, u32[]{:S(2)}, u32[]{:S(2)}) collective-permute-start(bf16[1,264,128]{2,1,0:T(8,128)(2,1)S(1)} %collective-permute-done.10.refs_12_), channel_id=1, source_target_pairs={{0,1},{1,0},{2,3},{3,2},{4,5},{5,4},{6,7},{7,6},{8,9},{9,8},{10,11... | collective-permute-start | bytes 202760 | tf_op jit(solution)/shard_map/ppermute | solution.py:40
  18.8 1.6 %collective-permute-done.14.refs_16_ = bf16[1,264,128]{2,1,0:T(8,128)(2,1)S(1)} collective-permute-done((bf16[1,264,128]{2,1,0:T(8,128)(2,1)S(1)}, bf16[1,264,128]{2,1,0:T(8,128)(2,1)S(1)}, u32[]{:S(2)}, u32[]{:S(2)}) %collective-permute-start.14) | collective-permute-done | bytes 67616 | tf_op jit(solution)/shard_map/ppermute | solution.py:40
  20.4 0.0 collective-permute-start.13
  20.4 0.0 collective-permute-done.7.refs_9_
  20.4 0.5 %collective-permute-start.15 = (bf16[1,264,128]{2,1,0:T(8,128)(2,1)S(1)}, bf16[1,264,128]{2,1,0:T(8,128)(2,1)S(1)}, u32[]{:S(2)}, u32[]{:S(2)}) collective-permute-start(bf16[1,264,128]{2,1,0:T(8,128)(2,1)S(1)} %collective-permute-done.14.refs_16_), channel_id=1, source_target_pairs={{0,1},{1,0},{2,3},{3,2},{4,5},{5,4},{6,7},{7,6},{8,9},{9,8},{10,11... | collective-permute-start | bytes 202760 | tf_op jit(solution)/shard_map/ppermute | solution.py:40
  20.9 0.0 collective-permute-done.9.refs_11_
  20.9 0.0 collective-permute-done.11.refs_13_
  20.9 0.7 %collective-permute-done.13.refs_15_ = bf16[1,264,128]{2,1,0:T(8,128)(2,1)S(1)} collective-permute-done((bf16[1,264,128]{2,1,0:T(8,128)(2,1)S(1)}, bf16[1,264,128]{2,1,0:T(8,128)(2,1)S(1)}, u32[]{:S(2)}, u32[]{:S(2)}) %collective-permute-start.13) | collective-permute-done | bytes 67616 | tf_op jit(solution)/shard_map/ppermute | solution.py:40
  21.6 0.2 collective-permute-done.15.refs_17_
  21.8 0.0 collective-permute-done.refs_1_
  21.8 4.6 %shard_map.93 = (bf16[1,32,8,128]{3,2,1,0:T(8,128)(2,1)S(1)}, bf16[1,32,8,128]{3,2,1,0:T(8,128)(2,1)S(1)}, bf16[1,32,8,128]{3,2,1,0:T(8,128)(2,1)S(1)}, bf16[1,32,8,128]{3,2,1,0:T(8,128)(2,1)S(1)}) custom-call(bf16[96,1280]{1,0:T(8,128)(2,1)S(1)} %shard_map.91.refs_0_, bf16[96,1280]{1,0:T(8,128)(2,1)S(1)} %collective-permute-done.refs_1_, ...), custom_call_target="tpu_custom_call" | custom-call | tf_op jit(solution)/shard_map/pallas_call | solution.py:61
  26.4 0.9 %collective-permute-start.16 = (bf16[1,32,8,128]{3,2,1,0:T(8,128)(2,1)S(1)}, bf16[1,32,8,128]{3,2,1,0:T(8,128)(2,1)S(1)}, u32[]{:S(2)}, u32[]{:S(2)}) collective-permute-start(bf16[1,32,8,128]{3,2,1,0:T(8,128)(2,1)S(1)} %get-tuple-element.18), channel_id=1, source_target_pairs={{0,4},{4,8},{8,12},{12,0},{1,5},{5,9},{9,13},{13,1},{2,6},{6,10},{... | collective-permute-start | bytes 196616 | tf_op jit(solution)/shard_map/ppermute | solution.py:40
  27.3 2.7 %collective-permute-start.17 = (bf16[1,32,8,128]{3,2,1,0:T(8,128)(2,1)S(1)}, bf16[1,32,8,128]{3,2,1,0:T(8,128)(2,1)S(1)}, u32[]{:S(2)}, u32[]{:S(2)}) collective-permute-start(bf16[1,32,8,128]{3,2,1,0:T(8,128)(2,1)S(1)} %get-tuple-element.19), channel_id=1, source_target_pairs={{0,8},{4,12},{8,0},{12,4},{1,9},{5,13},{9,1},{13,5},{2,10},{6,14},... | collective-permute-start | bytes 196616 | tf_op jit(solution)/shard_map/ppermute | solution.py:40
  30.0 0.3 collective-permute-start.18
  30.2 3.0 %collective-permute-done.16.refs_1_ = bf16[1,32,8,128]{3,2,1,0:T(8,128)(2,1)S(1)} collective-permute-done((bf16[1,32,8,128]{3,2,1,0:T(8,128)(2,1)S(1)}, bf16[1,32,8,128]{3,2,1,0:T(8,128)(2,1)S(1)}, u32[]{:S(2)}, u32[]{:S(2)}) %collective-permute-start.16) | collective-permute-done | bytes 65568 | tf_op jit(solution)/shard_map/ppermute | solution.py:40
  33.3 2.2 %collective-permute-done.17.refs_2_ = bf16[1,32,8,128]{3,2,1,0:T(8,128)(2,1)S(1)} collective-permute-done((bf16[1,32,8,128]{3,2,1,0:T(8,128)(2,1)S(1)}, bf16[1,32,8,128]{3,2,1,0:T(8,128)(2,1)S(1)}, u32[]{:S(2)}, u32[]{:S(2)}) %collective-permute-start.17) | collective-permute-done | bytes 65568 | tf_op jit(solution)/shard_map/ppermute | solution.py:40
  35.5 0.0 collective-permute-done.18.refs_3_
  35.5 0.7 %shard_map.94 = bf16[4,1,32,8,128]{4,3,2,1,0:T(8,128)(2,1)} custom-call(bf16[1,32,8,128]{3,2,1,0:T(8,128)(2,1)S(1)} %get-tuple-element.17.refs_0_, bf16[1,32,8,128]{3,2,1,0:T(8,128)(2,1)S(1)} %collective-permute-done.16.refs_1_, bf16[1,32,8,128]{3,2,1,0:T(8,128)(2,1)S(1)} %collective-permute-done.17.refs_2_, ...), custom_call_target="tpu_custom_call" | custom-call | tf_op jit(solution)/shard_map/pallas_call | solution.py:61
Async XLA Ops:
  1.1 9.9 %collective-permute-start.2 = (bf16[1,264,128]{2,1,0:T(8,128)(2,1)S(1)}, bf16[1,264,128]{2,1,0:T(8,128)(2,1)S(1)}, u32[]{:S(2)}, u32[]{:S(2)}) collective-permute-start(bf16[1,264,128]{2,1,0:T(8,128)(2,1)S(1)} %get-tuple-element.14), channel_id=1, source_target_pairs={{0,4},{4,8},{8,12},{12,0},{1,5},{5,9},{9,13},{13,1},{2,6},{6,10},{... | collective-permute-start | bytes 202760 | tf_op jit(solution)/shard_map/ppermute | solution.py:40
  4.2 7.2 %collective-permute-start.4 = (bf16[1,264,128]{2,1,0:T(8,128)(2,1)S(1)}, bf16[1,264,128]{2,1,0:T(8,128)(2,1)S(1)}, u32[]{:S(2)}, u32[]{:S(2)}) collective-permute-start(bf16[1,264,128]{2,1,0:T(8,128)(2,1)S(1)} %get-tuple-element.15), channel_id=1, source_target_pairs={{0,8},{4,12},{8,0},{12,4},{1,9},{5,13},{9,1},{13,5},{2,10},{6,14},... | collective-permute-start | bytes 202760 | tf_op jit(solution)/shard_map/ppermute | solution.py:40
  6.8 6.3 %collective-permute-start.6 = (bf16[1,264,128]{2,1,0:T(8,128)(2,1)S(1)}, bf16[1,264,128]{2,1,0:T(8,128)(2,1)S(1)}, u32[]{:S(2)}, u32[]{:S(2)}) collective-permute-start(bf16[1,264,128]{2,1,0:T(8,128)(2,1)S(1)} %get-tuple-element.16), channel_id=1, source_target_pairs={{0,12},{4,0},{8,4},{12,8},{1,13},{5,1},{9,5},{13,9},{2,14},{6,2},{... | collective-permute-start | bytes 202760 | tf_op jit(solution)/shard_map/ppermute | solution.py:40
  9.3 12.4 %collective-permute-start = (bf16[96,1280]{1,0:T(8,128)(2,1)S(1)}, bf16[96,1280]{1,0:T(8,128)(2,1)S(1)}, u32[]{:S(2)}, u32[]{:S(2)}) collective-permute-start(bf16[96,1280]{1,0:T(8,128)(2,1)S(1)} %shard_map.91.refs_0_), channel_id=1, source_target_pairs={{0,1},{1,0},{2,3},{3,2},{4,5},{5,4},{6,7},{7,6},{8,9},{9,8},{10,11... | collective-permute-start | bytes 737288 | tf_op jit(solution)/shard_map/ppermute | solution.py:40
  9.4 4.5 %collective-permute-start.8 = (bf16[1,264,128]{2,1,0:T(8,128)(2,1)S(1)}, bf16[1,264,128]{2,1,0:T(8,128)(2,1)S(1)}, u32[]{:S(2)}, u32[]{:S(2)}) collective-permute-start(bf16[1,264,128]{2,1,0:T(8,128)(2,1)S(1)} %get-tuple-element.13.refs_2_), channel_id=1, source_target_pairs={{0,2},{2,0},{1,3},{3,1},{4,6},{6,4},{5,7},{7,5},{8,10},{10,8},{9,1... | collective-permute-start | bytes 202760 | tf_op jit(solution)/shard_map/ppermute | solution.py:40
  11.0 4.8 %collective-permute-start.1 = (bf16[1,264,128]{2,1,0:T(8,128)(2,1)S(1)}, bf16[1,264,128]{2,1,0:T(8,128)(2,1)S(1)}, u32[]{:S(2)}, u32[]{:S(2)}) collective-permute-start(bf16[1,264,128]{2,1,0:T(8,128)(2,1)S(1)} %get-tuple-element.13.refs_2_), channel_id=1, source_target_pairs={{0,1},{1,0},{2,3},{3,2},{4,5},{5,4},{6,7},{7,6},{8,9},{9,8},{10,11... | collective-permute-start | bytes 202760 | tf_op jit(solution)/shard_map/ppermute | solution.py:40
  11.4 4.4 %collective-permute-start.10 = (bf16[1,264,128]{2,1,0:T(8,128)(2,1)S(1)}, bf16[1,264,128]{2,1,0:T(8,128)(2,1)S(1)}, u32[]{:S(2)}, u32[]{:S(2)}) collective-permute-start(bf16[1,264,128]{2,1,0:T(8,128)(2,1)S(1)} %collective-permute-done.2.refs_4_), channel_id=1, source_target_pairs={{0,2},{2,0},{1,3},{3,1},{4,6},{6,4},{5,7},{7,5},{8,10},{10,8},{9,1... | collective-permute-start | bytes 202760 | tf_op jit(solution)/shard_map/ppermute | solution.py:40
  13.1 4.3 %collective-permute-start.3 = (bf16[1,264,128]{2,1,0:T(8,128)(2,1)S(1)}, bf16[1,264,128]{2,1,0:T(8,128)(2,1)S(1)}, u32[]{:S(2)}, u32[]{:S(2)}) collective-permute-start(bf16[1,264,128]{2,1,0:T(8,128)(2,1)S(1)} %collective-permute-done.2.refs_4_), channel_id=1, source_target_pairs={{0,1},{1,0},{2,3},{3,2},{4,5},{5,4},{6,7},{7,6},{8,9},{9,8},{10,11... | collective-permute-start | bytes 202760 | tf_op jit(solution)/shard_map/ppermute | solution.py:40
  14.0 4.3 %collective-permute-start.12 = (bf16[1,264,128]{2,1,0:T(8,128)(2,1)S(1)}, bf16[1,264,128]{2,1,0:T(8,128)(2,1)S(1)}, u32[]{:S(2)}, u32[]{:S(2)}) collective-permute-start(bf16[1,264,128]{2,1,0:T(8,128)(2,1)S(1)} %collective-permute-done.4.refs_6_), channel_id=1, source_target_pairs={{0,2},{2,0},{1,3},{3,1},{4,6},{6,4},{5,7},{7,5},{8,10},{10,8},{9,1... | collective-permute-start | bytes 202760 | tf_op jit(solution)/shard_map/ppermute | solution.py:40
  15.8 2.4 %collective-permute-start.5 = (bf16[1,264,128]{2,1,0:T(8,128)(2,1)S(1)}, bf16[1,264,128]{2,1,0:T(8,128)(2,1)S(1)}, u32[]{:S(2)}, u32[]{:S(2)}) collective-permute-start(bf16[1,264,128]{2,1,0:T(8,128)(2,1)S(1)} %collective-permute-done.4.refs_6_), channel_id=1, source_target_pairs={{0,1},{1,0},{2,3},{3,2},{4,5},{5,4},{6,7},{7,6},{8,9},{9,8},{10,11... | collective-permute-start | bytes 202760 | tf_op jit(solution)/shard_map/ppermute | solution.py:40
  15.8 4.5 %collective-permute-start.14 = (bf16[1,264,128]{2,1,0:T(8,128)(2,1)S(1)}, bf16[1,264,128]{2,1,0:T(8,128)(2,1)S(1)}, u32[]{:S(2)}, u32[]{:S(2)}) collective-permute-start(bf16[1,264,128]{2,1,0:T(8,128)(2,1)S(1)} %collective-permute-done.6.refs_8_), channel_id=1, source_target_pairs={{0,2},{2,0},{1,3},{3,1},{4,6},{6,4},{5,7},{7,5},{8,10},{10,8},{9,1... | collective-permute-start | bytes 202760 | tf_op jit(solution)/shard_map/ppermute | solution.py:40
  17.4 3.0 %collective-permute-start.7 = (bf16[1,264,128]{2,1,0:T(8,128)(2,1)S(1)}, bf16[1,264,128]{2,1,0:T(8,128)(2,1)S(1)}, u32[]{:S(2)}, u32[]{:S(2)}) collective-permute-start(bf16[1,264,128]{2,1,0:T(8,128)(2,1)S(1)} %collective-permute-done.6.refs_8_), channel_id=1, source_target_pairs={{0,1},{1,0},{2,3},{3,2},{4,5},{5,4},{6,7},{7,6},{8,9},{9,8},{10,11... | collective-permute-start | bytes 202760 | tf_op jit(solution)/shard_map/ppermute | solution.py:40
  18.3 2.6 %collective-permute-start.9 = (bf16[1,264,128]{2,1,0:T(8,128)(2,1)S(1)}, bf16[1,264,128]{2,1,0:T(8,128)(2,1)S(1)}, u32[]{:S(2)}, u32[]{:S(2)}) collective-permute-start(bf16[1,264,128]{2,1,0:T(8,128)(2,1)S(1)} %collective-permute-done.8.refs_10_), channel_id=1, source_target_pairs={{0,1},{1,0},{2,3},{3,2},{4,5},{5,4},{6,7},{7,6},{8,9},{9,8},{10,11... | collective-permute-start | bytes 202760 | tf_op jit(solution)/shard_map/ppermute | solution.py:40
  18.3 2.6 %collective-permute-start.11 = (bf16[1,264,128]{2,1,0:T(8,128)(2,1)S(1)}, bf16[1,264,128]{2,1,0:T(8,128)(2,1)S(1)}, u32[]{:S(2)}, u32[]{:S(2)}) collective-permute-start(bf16[1,264,128]{2,1,0:T(8,128)(2,1)S(1)} %collective-permute-done.10.refs_12_), channel_id=1, source_target_pairs={{0,1},{1,0},{2,3},{3,2},{4,5},{5,4},{6,7},{7,6},{8,9},{9,8},{10,11... | collective-permute-start | bytes 202760 | tf_op jit(solution)/shard_map/ppermute | solution.py:40
  20.4 1.3 %collective-permute-start.13 = (bf16[1,264,128]{2,1,0:T(8,128)(2,1)S(1)}, bf16[1,264,128]{2,1,0:T(8,128)(2,1)S(1)}, u32[]{:S(2)}, u32[]{:S(2)}) collective-permute-start(bf16[1,264,128]{2,1,0:T(8,128)(2,1)S(1)} %collective-permute-done.12.refs_14_), channel_id=1, source_target_pairs={{0,1},{1,0},{2,3},{3,2},{4,5},{5,4},{6,7},{7,6},{8,9},{9,8},{10,11... | collective-permute-start | bytes 202760 | tf_op jit(solution)/shard_map/ppermute | solution.py:40
  20.4 1.4 %collective-permute-start.15 = (bf16[1,264,128]{2,1,0:T(8,128)(2,1)S(1)}, bf16[1,264,128]{2,1,0:T(8,128)(2,1)S(1)}, u32[]{:S(2)}, u32[]{:S(2)}) collective-permute-start(bf16[1,264,128]{2,1,0:T(8,128)(2,1)S(1)} %collective-permute-done.14.refs_16_), channel_id=1, source_target_pairs={{0,1},{1,0},{2,3},{3,2},{4,5},{5,4},{6,7},{7,6},{8,9},{9,8},{10,11... | collective-permute-start | bytes 202760 | tf_op jit(solution)/shard_map/ppermute | solution.py:40
  26.4 6.9 %collective-permute-start.16 = (bf16[1,32,8,128]{3,2,1,0:T(8,128)(2,1)S(1)}, bf16[1,32,8,128]{3,2,1,0:T(8,128)(2,1)S(1)}, u32[]{:S(2)}, u32[]{:S(2)}) collective-permute-start(bf16[1,32,8,128]{3,2,1,0:T(8,128)(2,1)S(1)} %get-tuple-element.18), channel_id=1, source_target_pairs={{0,4},{4,8},{8,12},{12,0},{1,5},{5,9},{9,13},{13,1},{2,6},{6,10},{... | collective-permute-start | bytes 196616 | tf_op jit(solution)/shard_map/ppermute | solution.py:40
  27.3 8.2 %collective-permute-start.17 = (bf16[1,32,8,128]{3,2,1,0:T(8,128)(2,1)S(1)}, bf16[1,32,8,128]{3,2,1,0:T(8,128)(2,1)S(1)}, u32[]{:S(2)}, u32[]{:S(2)}) collective-permute-start(bf16[1,32,8,128]{3,2,1,0:T(8,128)(2,1)S(1)} %get-tuple-element.19), channel_id=1, source_target_pairs={{0,8},{4,12},{8,0},{12,4},{1,9},{5,13},{9,1},{13,5},{2,10},{6,14},... | collective-permute-start | bytes 196616 | tf_op jit(solution)/shard_map/ppermute | solution.py:40
  30.0 5.5 %collective-permute-start.18 = (bf16[1,32,8,128]{3,2,1,0:T(8,128)(2,1)S(1)}, bf16[1,32,8,128]{3,2,1,0:T(8,128)(2,1)S(1)}, u32[]{:S(2)}, u32[]{:S(2)}) collective-permute-start(bf16[1,32,8,128]{3,2,1,0:T(8,128)(2,1)S(1)} %get-tuple-element.20), channel_id=1, source_target_pairs={{0,12},{4,0},{8,4},{12,8},{1,13},{5,1},{9,5},{13,9},{2,14},{6,2},{... | collective-permute-start | bytes 196616 | tf_op jit(solution)/shard_map/ppermute | solution.py:40

commit v2 on v1

--- a/solution.py
+++ b/solution.py
@@ -48,7 +48,7 @@
     return tuple(pltpu.with_memory_space_constraint(array, pltpu.HBM) for array in arrays)
 
 
-def call(kernel, operands, out_shape, scratch, in_specs, out_specs):
+def call(kernel, operands, out_shape, scratch, in_specs, out_specs, aliases=None):
     shapes = jax.tree.leaves((operands, out_shape))
     held = sum(
         shape.size * shape.dtype.itemsize
@@ -64,6 +64,7 @@
         in_specs=in_specs,
         out_specs=out_specs,
         scratch_shapes=scratch,
+        input_output_aliases=aliases or {},
         compiler_params=pltpu.CompilerParams(vmem_limit_bytes=held + SPARE),
     )(*operands)
 
@@ -134,23 +135,23 @@
             outs[shift][index, part * depth :] = tail.astype(jnp.float32).astype(jnp.bfloat16)
 
 
-def unpack(*refs):
-    blocks, out, left = refs[:-2], refs[-2], refs[-1]
-    groups = len(blocks)
-    count = out.shape[0] // groups
+def unpack(turns, groups, *refs):
+    blocks, (out, stage, ready, left) = refs[: len(turns)], refs[-4:]
+    count, depth, part, cols = blocks[0].shape
+    tile = lax.axis_index("tiles")
     span = lax.axis_size("tiles") // groups
-    tile = lax.axis_index("tiles")
     copies = []
-    for turn, block in enumerate(blocks):
+    for place, (turn, block) in enumerate(zip(turns, blocks)):
         first = origin(tile // span, turn, groups) * count
         for index in range(count):
-            copies.append(
-                pltpu.make_async_copy(
-                    block.at[index], out.at[first + index, 0], left.at[turn * count + index]
-                )
-            )
-    for copy in copies:
-        copy.start()
+            slot = place * count + index
+            for row in range(depth):
+                value = block[index, row].astype(jnp.float32)
+                stage[slot, pl.ds(row, part, stride=depth), :] = value
+            ready[slot] = stage[slot].reshape(part, depth, cols).astype(jnp.bfloat16)
+            copy = pltpu.make_async_copy(ready.at[slot], out.at[first + index, 0], left.at[slot])
+            copy.start()
+            copies.append(copy)
     for copy in copies:
         copy.wait()
 
@@ -214,7 +215,7 @@
     sides, refs = refs[:chans], refs[chans:]
     blocks, refs = refs[:n_blocks], refs[n_blocks:]
     outs, refs = refs[:groups], refs[groups:]
-    weights, numbers, table, features, joined, inner, history, stage, counted = refs
+    weights, numbers, table, features, joined, inner, history, final, counted = refs
     channels = part * chans
     rows = tiles * depth
     tile, frame_here, chan = (lax.axis_index(name) for name in ("tiles", "frames", "chan"))
@@ -239,17 +240,18 @@
                     row * part : (row + 1) * part
                 ]
 
-    def bias_of(index):
-        block = weights[:channels, starts[-1] : starts[-1] + LANES].astype(jnp.float32)
+    def bias_of(matrix, index, many):
+        block = matrix[:many, starts[-1] : starts[-1] + LANES].astype(jnp.float32)
         lane = lax.broadcasted_iota(jnp.int32, block.shape, 1)
         mine = (lane >= PIECES * index) & (lane < PIECES * (index + 1))
         column = jnp.sum(jnp.where(mine, block, 0.0), axis=1, keepdims=True)
-        return jnp.broadcast_to(column, (channels, cols))
-
-    def convolve(inputs, index, emit):
+        return jnp.broadcast_to(column, (many, cols))
+
+    def convolve(inputs, index, emit, packed=weights):
         low = starts[index]
-        matrix = weights[:, low : low + TAPS * channels * len(inputs)]
-        bias = bias_of(index)
+        many = packed.shape[0] // TAPS
+        matrix = packed[:, low : low + TAPS * channels * len(inputs)]
+        bias = bias_of(packed, index, many)
 
         def step(turn, carried):
             above, here = carried
@@ -264,9 +266,9 @@
             )
             for row in range(GROUP):
                 one = partial[:, row * cols : (row + 1) * cols]
-                emit(first + row, above + one[2 * channels :])
-                above = here + one[channels : 2 * channels]
-                here = bias + one[:channels]
+                emit(first + row, above + one[2 * many :])
+                above = here + one[many : 2 * many]
+                here = bias + one[:many]
             return above, here
 
         turns = rows // GROUP
@@ -295,8 +297,9 @@
             numbers[block : block + 1, :] = tail[:1]
         to_table = pltpu.make_async_copy(numbers, table, counted)
         to_table.start()
-        for frame in range(frames):
-            def load_own(block, row, frame=frame):
+
+        def run(frame, segment):
+            def load_own(block, row):
                 first = pl.multiple_of(lax.rem(row, depth) * part, part)
                 pieces = [features[frame, side, block, pl.ds(first, part)] for side in range(chans)]
                 return jnp.concatenate(pieces, axis=0)
@@ -305,9 +308,9 @@
             for back, field in ((1, 2 * frame), (2, 2 * (frames + frame))):
                 if frame >= back:
                     inputs.append(displaced(history.at[(frame - back) % kept], field))
-            if frame == min(1, frames - 1):
-                to_table.wait()
-            new = history.at[frame % kept]
+            last = frame == frames - 1
+            new = final if last else history.at[frame % kept]
+            mine = pl.ds(pl.multiple_of(chan * part, part), part)
 
             def emit_join(slot, total):
                 joined[slot] = jnp.where(total > 0, total, 0.1 * total).astype(jnp.bfloat16)
@@ -315,26 +318,28 @@
             def emit_inner(slot, total):
                 inner[slot] = jnp.maximum(total, 0.0).astype(jnp.bfloat16)
 
-            def emit_second(slot, total, new=new):
-                state = joined[slot].astype(jnp.float32) + total
-                new[top - 1 + slot] = state.astype(jnp.bfloat16)
+            def emit_second(slot, total):
+                before = joined[slot, mine] if last else joined[slot]
+                new[top - 1 + slot] = (before.astype(jnp.float32) + total).astype(jnp.bfloat16)
 
             convolve(inputs, 0, emit_join)
             convolve([stored(joined)], 1, emit_inner)
-            convolve([stored(inner)], 2, emit_second)
-            new[top - 1] = jnp.zeros((channels, cols), jnp.bfloat16)
+            convolve([stored(inner)], 2, emit_second, sides[0] if last else weights)
+            if not last:
+                new[top - 1] = jnp.zeros((channels, cols), jnp.bfloat16)
 
             @pl.when(frame_here == frame)
-            def _(segment=segment, new=new):
+            def _():
                 for turn in range(groups):
                     target = partner(tile // span, turn, groups) * span + lax.rem(tile, span)
                     for row in range(depth):
-                        value = new[
-                            top + target * depth + row, pl.ds(pl.multiple_of(chan * part, part), part)
-                        ]
-                        stage[turn, pl.ds(row, part, stride=depth), :] = value.astype(jnp.float32)
-                    whole = stage[turn].reshape(part, depth, cols)
-                    outs[turn][segment] = whole.astype(jnp.bfloat16)
+                        at = top + target * depth + row
+                        outs[turn][segment, row] = new[at] if last else new[at, mine]
+
+        run(0, segment)
+        to_table.wait()
+        for frame in range(1, frames):
+            pl.when(frame_here >= frame)(functools.partial(run, frame, segment))
 
 
 def shards(lr_feats, flow_prev, flow_second, w_join, b_join, w_first, b_first, w_second, b_second):
@@ -389,7 +394,7 @@
     outs = call(
         functools.partial(recurrence, (frames, tiles, chans, segments, part, depth, cols), widths),
         (*sides, *blocks),
-        [jax.ShapeDtypeStruct((count, part, depth, cols), jnp.bfloat16)] * groups,
+        [jax.ShapeDtypeStruct((count, depth, part, cols), jnp.bfloat16)] * groups,
         [
             pltpu.VMEM((TAPS * channels, wide), jnp.bfloat16),
             pltpu.VMEM((tiles, cols), jnp.int32),
@@ -398,7 +403,7 @@
             pltpu.VMEM((rows + 1, channels, cols), jnp.bfloat16),
             pltpu.VMEM((rows + 1, channels, cols), jnp.bfloat16),
             pltpu.VMEM((kept, rows + 2 * depth + 1, channels, cols), jnp.bfloat16),
-            pltpu.VMEM((groups, part * depth, cols), jnp.float32),
+            pltpu.VMEM((rows + 2 * depth + 1, part, cols), jnp.bfloat16),
             pltpu.SemaphoreType.DMA(()),
         ],
         [VMEM] * (chans + len(blocks)),
@@ -407,14 +412,27 @@
     returned = {0: outs[0]}
     for turn in ranked(groups):
         returned[turn] = hop(outs[turn], "tiles", turn, span)
-    return call(
-        unpack,
-        tuple(returned[turn] for turn in range(groups)),
-        jax.ShapeDtypeStruct(lr_feats.shape, lr_feats.dtype),
-        [pltpu.SemaphoreType.DMA((segments,))],
-        [VMEM] * groups,
-        HBM,
-    )
+    turns = [0] + ranked(groups)
+    result = ()
+    for some in (turns[: groups // 2], turns[groups // 2 :]):
+        if some:
+            slots = len(some) * count
+            result = (
+                call(
+                    functools.partial(unpack, some, groups),
+                    tuple(returned[turn] for turn in some) + result,
+                    jax.ShapeDtypeStruct(lr_feats.shape, lr_feats.dtype),
+                    [
+                        pltpu.VMEM((slots, part * depth, cols), jnp.float32),
+                        pltpu.VMEM((slots, part, depth, cols), jnp.bfloat16),
+                        pltpu.SemaphoreType.DMA((slots,)),
+                    ],
+                    [VMEM] * len(some) + [HBM] * len(result),
+                    HBM,
+                    {len(some): 0} if result else None,
+                ),
+            )
+    return result[0]
 
 
 def solution(mesh):

time: 36.4 us -> 35.2 us (0.967)
  the two profiles are of different devices: /device:TPU:0 before, /device:TPU:11 now
where the time goes in v2:
time: 35.2 us; the launch traced here: 35 us
  starting transfers between devices  20 us (57%)
  Pallas kernels  8.1 us (23%)
  waiting for transfers between devices  6.92 us (20%)
    ppermute x19, starting transfers between devices, hop(): return lax.ppermute(array, axis, pairs)  20 us
    pallas_call x5, Pallas kernels, call(): pl.pallas_call(kernel, out_shape=out_shape, in_specs=in_specs, out_specs=...  8.1 us
    ppermute x19, waiting for transfers between devices, hop(): return lax.ppermute(array, axis, pairs)  6.92 us
  transfers between devices with their start and end apart: 19, of which 8 were waited for; matrix products, arithmetic and copies ran while one was open for 0% of the time, Pallas kernels for 6%

profile of v2, /device:TPU:11, one launch (start us, length us, event | category | flops | bytes accessed | tf_op | source)
XLA Modules:
  0.0 35.0 jit_solution(18391788265387694749)
XLA Ops:
  0.0 1.1 %shard_map.92 = (bf16[1,264,128]{2,1,0:T(8,128)(2,1)S(1)}, bf16[1,264,128]{2,1,0:T(8,128)(2,1)S(1)}, bf16[1,264,128]{2,1,0:T(8,128)(2,1)S(1)}, bf16[1,264,128]{2,1,0:T(8,128)(2,1)S(1)}) custom-call(bf16[4,1,32,8,128]{4,3,2,1,0:T(8,128)(2,1)} %lr_feats.1, s32[2,1,2,4]{3,2,1,0:T(2,128)} %bitcast.7, s32[2,1,2,4]{3,2,1,0:T(2,128)} %bitcast.8), custom_call_target="tpu_custom_call" | custom-call | tf_op jit(solution)/shard_map/pallas_call | solution.py:61
  1.1 1.3 %collective-permute-start.2 = (bf16[1,264,128]{2,1,0:T(8,128)(2,1)S(1)}, bf16[1,264,128]{2,1,0:T(8,128)(2,1)S(1)}, u32[]{:S(2)}, u32[]{:S(2)}) collective-permute-start(bf16[1,264,128]{2,1,0:T(8,128)(2,1)S(1)} %get-tuple-element.14), channel_id=1, source_target_pairs={{0,4},{4,8},{8,12},{12,0},{1,5},{5,9},{9,13},{13,1},{2,6},{6,10},{... | collective-permute-start | bytes 202760 | tf_op jit(solution)/shard_map/ppermute | solution.py:40
  2.4 1.1 %collective-permute-start.4 = (bf16[1,264,128]{2,1,0:T(8,128)(2,1)S(1)}, bf16[1,264,128]{2,1,0:T(8,128)(2,1)S(1)}, u32[]{:S(2)}, u32[]{:S(2)}) collective-permute-start(bf16[1,264,128]{2,1,0:T(8,128)(2,1)S(1)} %get-tuple-element.15), channel_id=1, source_target_pairs={{0,8},{4,12},{8,0},{12,4},{1,9},{5,13},{9,1},{13,5},{2,10},{6,14},... | collective-permute-start | bytes 202760 | tf_op jit(solution)/shard_map/ppermute | solution.py:40
  3.5 1.4 %collective-permute-start.6 = (bf16[1,264,128]{2,1,0:T(8,128)(2,1)S(1)}, bf16[1,264,128]{2,1,0:T(8,128)(2,1)S(1)}, u32[]{:S(2)}, u32[]{:S(2)}) collective-permute-start(bf16[1,264,128]{2,1,0:T(8,128)(2,1)S(1)} %get-tuple-element.16), channel_id=1, source_target_pairs={{0,12},{4,0},{8,4},{12,8},{1,13},{5,1},{9,5},{13,9},{2,14},{6,2},{... | collective-permute-start | bytes 202760 | tf_op jit(solution)/shard_map/ppermute | solution.py:40
  4.9 1.2 %shard_map.91.refs_0_ = bf16[96,1280]{1,0:T(8,128)(2,1)S(1)} custom-call(bf16[9,32,192]{2,1,0:T(8,128)(2,1)} %refs_0_.1, bf16[9,32,64]{2,1,0:T(8,128)(2,1)} %bitcast.5, bf16[9,32,64]{2,1,0:T(8,128)(2,1)} %bitcast.6, f32[1,32]{1,0:T(1,128)} %bitcast.9, f32[1,32]{1,0:T(1,128)} %refs_4_.1, f32[1,32]{1,0:T(1,128)} %refs_5_.1), custom_call_target="tpu_custom_call" | custom-call | tf_op jit(solution)/shard_map/pallas_call | solution.py:61
  6.1 1.6 %collective-permute-start = (bf16[96,1280]{1,0:T(8,128)(2,1)S(1)}, bf16[96,1280]{1,0:T(8,128)(2,1)S(1)}, u32[]{:S(2)}, u32[]{:S(2)}) collective-permute-start(bf16[96,1280]{1,0:T(8,128)(2,1)S(1)} %shard_map.91.refs_0_), channel_id=1, source_target_pairs={{0,1},{1,0},{2,3},{3,2},{4,5},{5,4},{6,7},{7,6},{8,9},{9,8},{10,11... | collective-permute-start | bytes 737288 | tf_op jit(solution)/shard_map/ppermute | solution.py:40
  7.7 0.3 collective-permute-start.8
  8.0 0.0 collective-permute-done.2.refs_4_
  8.0 0.4 %collective-permute-start.1 = (bf16[1,264,128]{2,1,0:T(8,128)(2,1)S(1)}, bf16[1,264,128]{2,1,0:T(8,128)(2,1)S(1)}, u32[]{:S(2)}, u32[]{:S(2)}) collective-permute-start(bf16[1,264,128]{2,1,0:T(8,128)(2,1)S(1)} %get-tuple-element.13.refs_2_), channel_id=1, source_target_pairs={{0,1},{1,0},{2,3},{3,2},{4,5},{5,4},{6,7},{7,6},{8,9},{9,8},{10,11... | collective-permute-start | bytes 202760 | tf_op jit(solution)/shard_map/ppermute | solution.py:40
  8.3 0.0 collective-permute-done.4.refs_6_
  8.3 1.2 %collective-permute-start.10 = (bf16[1,264,128]{2,1,0:T(8,128)(2,1)S(1)}, bf16[1,264,128]{2,1,0:T(8,128)(2,1)S(1)}, u32[]{:S(2)}, u32[]{:S(2)}) collective-permute-start(bf16[1,264,128]{2,1,0:T(8,128)(2,1)S(1)} %collective-permute-done.2.refs_4_), channel_id=1, source_target_pairs={{0,2},{2,0},{1,3},{3,1},{4,6},{6,4},{5,7},{7,5},{8,10},{10,8},{9,1... | collective-permute-start | bytes 202760 | tf_op jit(solution)/shard_map/ppermute | solution.py:40
  9.5 0.6 %collective-permute-done.6.refs_8_ = bf16[1,264,128]{2,1,0:T(8,128)(2,1)S(1)} collective-permute-done((bf16[1,264,128]{2,1,0:T(8,128)(2,1)S(1)}, bf16[1,264,128]{2,1,0:T(8,128)(2,1)S(1)}, u32[]{:S(2)}, u32[]{:S(2)}) %collective-permute-start.6) | collective-permute-done | bytes 67616 | tf_op jit(solution)/shard_map/ppermute | solution.py:40
  10.1 0.7 %collective-permute-start.3 = (bf16[1,264,128]{2,1,0:T(8,128)(2,1)S(1)}, bf16[1,264,128]{2,1,0:T(8,128)(2,1)S(1)}, u32[]{:S(2)}, u32[]{:S(2)}) collective-permute-start(bf16[1,264,128]{2,1,0:T(8,128)(2,1)S(1)} %collective-permute-done.2.refs_4_), channel_id=1, source_target_pairs={{0,1},{1,0},{2,3},{3,2},{4,5},{5,4},{6,7},{7,6},{8,9},{9,8},{10,11... | collective-permute-start | bytes 202760 | tf_op jit(solution)/shard_map/ppermute | solution.py:40
  10.9 0.4 %collective-permute-done.8.refs_10_ = bf16[1,264,128]{2,1,0:T(8,128)(2,1)S(1)} collective-permute-done((bf16[1,264,128]{2,1,0:T(8,128)(2,1)S(1)}, bf16[1,264,128]{2,1,0:T(8,128)(2,1)S(1)}, u32[]{:S(2)}, u32[]{:S(2)}) %collective-permute-start.8) | collective-permute-done | bytes 67616 | tf_op jit(solution)/shard_map/ppermute | solution.py:40
  11.3 0.3 collective-permute-start.12
  11.6 0.0 collective-permute-done.1.refs_3_
  11.6 1.2 %collective-permute-start.5 = (bf16[1,264,128]{2,1,0:T(8,128)(2,1)S(1)}, bf16[1,264,128]{2,1,0:T(8,128)(2,1)S(1)}, u32[]{:S(2)}, u32[]{:S(2)}) collective-permute-start(bf16[1,264,128]{2,1,0:T(8,128)(2,1)S(1)} %collective-permute-done.4.refs_6_), channel_id=1, source_target_pairs={{0,1},{1,0},{2,3},{3,2},{4,5},{5,4},{6,7},{7,6},{8,9},{9,8},{10,11... | collective-permute-start | bytes 202760 | tf_op jit(solution)/shard_map/ppermute | solution.py:40
  12.8 0.0 collective-permute-done.10.refs_12_
  12.8 1.7 %collective-permute-start.14 = (bf16[1,264,128]{2,1,0:T(8,128)(2,1)S(1)}, bf16[1,264,128]{2,1,0:T(8,128)(2,1)S(1)}, u32[]{:S(2)}, u32[]{:S(2)}) collective-permute-start(bf16[1,264,128]{2,1,0:T(8,128)(2,1)S(1)} %collective-permute-done.6.refs_8_), channel_id=1, source_target_pairs={{0,2},{2,0},{1,3},{3,1},{4,6},{6,4},{5,7},{7,5},{8,10},{10,8},{9,1... | collective-permute-start | bytes 202760 | tf_op jit(solution)/shard_map/ppermute | solution.py:40
  14.6 0.0 collective-permute-done.3.refs_5_
  14.6 0.3 collective-permute-start.7
  14.9 0.0 collective-permute-done.12.refs_14_
  14.9 2.7 %collective-permute-start.9 = (bf16[1,264,128]{2,1,0:T(8,128)(2,1)S(1)}, bf16[1,264,128]{2,1,0:T(8,128)(2,1)S(1)}, u32[]{:S(2)}, u32[]{:S(2)}) collective-permute-start(bf16[1,264,128]{2,1,0:T(8,128)(2,1)S(1)} %collective-permute-done.8.refs_10_), channel_id=1, source_target_pairs={{0,1},{1,0},{2,3},{3,2},{4,5},{5,4},{6,7},{7,6},{8,9},{9,8},{10,11... | collective-permute-start | bytes 202760 | tf_op jit(solution)/shard_map/ppermute | solution.py:40
  17.6 0.0 collective-permute-done.5.refs_7_
  17.7 0.0 collective-permute-start.11
  17.7 0.0 collective-permute-done.14.refs_16_
  17.7 0.7 %collective-permute-start.13 = (bf16[1,264,128]{2,1,0:T(8,128)(2,1)S(1)}, bf16[1,264,128]{2,1,0:T(8,128)(2,1)S(1)}, u32[]{:S(2)}, u32[]{:S(2)}) collective-permute-start(bf16[1,264,128]{2,1,0:T(8,128)(2,1)S(1)} %collective-permute-done.12.refs_14_), channel_id=1, source_target_pairs={{0,1},{1,0},{2,3},{3,2},{4,5},{5,4},{6,7},{7,6},{8,9},{9,8},{10,11... | collective-permute-start | bytes 202760 | tf_op jit(solution)/shard_map/ppermute | solution.py:40
  18.4 0.0 collective-permute-done.7.refs_9_
  18.4 0.0 collective-permute-start.15
  18.4 0.2 collective-permute-done.9.refs_11_
  18.6 0.4 %collective-permute-done.11.refs_13_ = bf16[1,264,128]{2,1,0:T(8,128)(2,1)S(1)} collective-permute-done((bf16[1,264,128]{2,1,0:T(8,128)(2,1)S(1)}, bf16[1,264,128]{2,1,0:T(8,128)(2,1)S(1)}, u32[]{:S(2)}, u32[]{:S(2)}) %collective-permute-start.11) | collective-permute-done | bytes 67616 | tf_op jit(solution)/shard_map/ppermute | solution.py:40
  18.9 0.4 %collective-permute-done.13.refs_15_ = bf16[1,264,128]{2,1,0:T(8,128)(2,1)S(1)} collective-permute-done((bf16[1,264,128]{2,1,0:T(8,128)(2,1)S(1)}, bf16[1,264,128]{2,1,0:T(8,128)(2,1)S(1)}, u32[]{:S(2)}, u32[]{:S(2)}) %collective-permute-start.13) | collective-permute-done | bytes 67616 | tf_op jit(solution)/shard_map/ppermute | solution.py:40
  19.3 0.4 %collective-permute-done.15.refs_17_ = bf16[1,264,128]{2,1,0:T(8,128)(2,1)S(1)} collective-permute-done((bf16[1,264,128]{2,1,0:T(8,128)(2,1)S(1)}, bf16[1,264,128]{2,1,0:T(8,128)(2,1)S(1)}, u32[]{:S(2)}, u32[]{:S(2)}) %collective-permute-start.15) | collective-permute-done | bytes 67616 | tf_op jit(solution)/shard_map/ppermute | solution.py:40
  19.6 0.0 collective-permute-done.refs_1_
  19.6 4.4 %shard_map.93 = (bf16[1,8,32,128]{3,2,1,0:T(8,128)(2,1)S(1)}, bf16[1,8,32,128]{3,2,1,0:T(8,128)(2,1)S(1)}, bf16[1,8,32,128]{3,2,1,0:T(8,128)(2,1)S(1)}, bf16[1,8,32,128]{3,2,1,0:T(8,128)(2,1)S(1)}) custom-call(bf16[96,1280]{1,0:T(8,128)(2,1)S(1)} %shard_map.91.refs_0_, bf16[96,1280]{1,0:T(8,128)(2,1)S(1)} %collective-permute-done.refs_1_, ...), custom_call_target="tpu_custom_call" | custom-call | tf_op jit(solution)/shard_map/pallas_call | solution.py:61
  24.0 0.7 %collective-permute-start.18 = (bf16[1,8,32,128]{3,2,1,0:T(8,128)(2,1)S(1)}, bf16[1,8,32,128]{3,2,1,0:T(8,128)(2,1)S(1)}, u32[]{:S(2)}, u32[]{:S(2)}) collective-permute-start(bf16[1,8,32,128]{3,2,1,0:T(8,128)(2,1)S(1)} %get-tuple-element.20), channel_id=1, source_target_pairs={{0,4},{4,8},{8,12},{12,0},{1,5},{5,9},{9,13},{13,1},{2,6},{6,10},{... | collective-permute-start | bytes 196616 | tf_op jit(solution)/shard_map/ppermute | solution.py:40
  24.7 2.9 %collective-permute-start.16 = (bf16[1,8,32,128]{3,2,1,0:T(8,128)(2,1)S(1)}, bf16[1,8,32,128]{3,2,1,0:T(8,128)(2,1)S(1)}, u32[]{:S(2)}, u32[]{:S(2)}) collective-permute-start(bf16[1,8,32,128]{3,2,1,0:T(8,128)(2,1)S(1)} %get-tuple-element.17), channel_id=1, source_target_pairs={{0,8},{4,12},{8,0},{12,4},{1,9},{5,13},{9,1},{13,5},{2,10},{6,14},... | collective-permute-start | bytes 196616 | tf_op jit(solution)/shard_map/ppermute | solution.py:40
  27.6 1.4 %collective-permute-start.17 = (bf16[1,8,32,128]{3,2,1,0:T(8,128)(2,1)S(1)}, bf16[1,8,32,128]{3,2,1,0:T(8,128)(2,1)S(1)}, u32[]{:S(2)}, u32[]{:S(2)}) collective-permute-start(bf16[1,8,32,128]{3,2,1,0:T(8,128)(2,1)S(1)} %get-tuple-element.18), channel_id=1, source_target_pairs={{0,12},{4,0},{8,4},{12,8},{1,13},{5,1},{9,5},{13,9},{2,14},{6,2},{... | collective-permute-start | bytes 196616 | tf_op jit(solution)/shard_map/ppermute | solution.py:40
  29.0 0.0 collective-permute-done.18.refs_1_
  29.0 0.7 %shard_map.94.refs_2_ = bf16[4,1,32,8,128]{4,3,2,1,0:T(8,128)(2,1)} custom-call(bf16[1,8,32,128]{3,2,1,0:T(8,128)(2,1)S(1)} %get-tuple-element.19.refs_0_, bf16[1,8,32,128]{3,2,1,0:T(8,128)(2,1)S(1)} %collective-permute-done.18.refs_1_), custom_call_target="tpu_custom_call" | custom-call | tf_op jit(solution)/shard_map/pallas_call | solution.py:61
  29.7 1.5 %collective-permute-done.16.refs_0_ = bf16[1,8,32,128]{3,2,1,0:T(8,128)(2,1)S(1)} collective-permute-done((bf16[1,8,32,128]{3,2,1,0:T(8,128)(2,1)S(1)}, bf16[1,8,32,128]{3,2,1,0:T(8,128)(2,1)S(1)}, u32[]{:S(2)}, u32[]{:S(2)}) %collective-permute-start.16) | collective-permute-done | bytes 65568 | tf_op jit(solution)/shard_map/ppermute | solution.py:40
  31.2 3.1 %collective-permute-done.17.refs_1_ = bf16[1,8,32,128]{3,2,1,0:T(8,128)(2,1)S(1)} collective-permute-done((bf16[1,8,32,128]{3,2,1,0:T(8,128)(2,1)S(1)}, bf16[1,8,32,128]{3,2,1,0:T(8,128)(2,1)S(1)}, u32[]{:S(2)}, u32[]{:S(2)}) %collective-permute-start.17) | collective-permute-done | bytes 65568 | tf_op jit(solution)/shard_map/ppermute | solution.py:40
  34.3 0.7 %shard_map.95 = bf16[4,1,32,8,128]{4,3,2,1,0:T(8,128)(2,1)} custom-call(bf16[1,8,32,128]{3,2,1,0:T(8,128)(2,1)S(1)} %collective-permute-done.16.refs_0_, bf16[1,8,32,128]{3,2,1,0:T(8,128)(2,1)S(1)} %collective-permute-done.17.refs_1_, bf16[4,1,32,8,128]{4,3,2,1,0:T(8,128)(2,1)} %shard_map.94.refs_2_), custom_call_target="tpu_custom_call", output_to_operand_aliasing={{}: (2, {})} | custom-call | tf_op jit(solution)/shard_map/pallas_call | solution.py:61
Async XLA Ops:
  1.1 6.9 %collective-permute-start.2 = (bf16[1,264,128]{2,1,0:T(8,128)(2,1)S(1)}, bf16[1,264,128]{2,1,0:T(8,128)(2,1)S(1)}, u32[]{:S(2)}, u32[]{:S(2)}) collective-permute-start(bf16[1,264,128]{2,1,0:T(8,128)(2,1)S(1)} %get-tuple-element.14), channel_id=1, source_target_pairs={{0,4},{4,8},{8,12},{12,0},{1,5},{5,9},{9,13},{13,1},{2,6},{6,10},{... | collective-permute-start | bytes 202760 | tf_op jit(solution)/shard_map/ppermute | solution.py:40
  2.4 5.9 %collective-permute-start.4 = (bf16[1,264,128]{2,1,0:T(8,128)(2,1)S(1)}, bf16[1,264,128]{2,1,0:T(8,128)(2,1)S(1)}, u32[]{:S(2)}, u32[]{:S(2)}) collective-permute-start(bf16[1,264,128]{2,1,0:T(8,128)(2,1)S(1)} %get-tuple-element.15), channel_id=1, source_target_pairs={{0,8},{4,12},{8,0},{12,4},{1,9},{5,13},{9,1},{13,5},{2,10},{6,14},... | collective-permute-start | bytes 202760 | tf_op jit(solution)/shard_map/ppermute | solution.py:40
  3.5 6.6 %collective-permute-start.6 = (bf16[1,264,128]{2,1,0:T(8,128)(2,1)S(1)}, bf16[1,264,128]{2,1,0:T(8,128)(2,1)S(1)}, u32[]{:S(2)}, u32[]{:S(2)}) collective-permute-start(bf16[1,264,128]{2,1,0:T(8,128)(2,1)S(1)} %get-tuple-element.16), channel_id=1, source_target_pairs={{0,12},{4,0},{8,4},{12,8},{1,13},{5,1},{9,5},{13,9},{2,14},{6,2},{... | collective-permute-start | bytes 202760 | tf_op jit(solution)/shard_map/ppermute | solution.py:40
  6.1 13.5 %collective-permute-start = (bf16[96,1280]{1,0:T(8,128)(2,1)S(1)}, bf16[96,1280]{1,0:T(8,128)(2,1)S(1)}, u32[]{:S(2)}, u32[]{:S(2)}) collective-permute-start(bf16[96,1280]{1,0:T(8,128)(2,1)S(1)} %shard_map.91.refs_0_), channel_id=1, source_target_pairs={{0,1},{1,0},{2,3},{3,2},{4,5},{5,4},{6,7},{7,6},{8,9},{9,8},{10,11... | collective-permute-start | bytes 737288 | tf_op jit(solution)/shard_map/ppermute | solution.py:40
  7.7 3.6 %collective-permute-start.8 = (bf16[1,264,128]{2,1,0:T(8,128)(2,1)S(1)}, bf16[1,264,128]{2,1,0:T(8,128)(2,1)S(1)}, u32[]{:S(2)}, u32[]{:S(2)}) collective-permute-start(bf16[1,264,128]{2,1,0:T(8,128)(2,1)S(1)} %get-tuple-element.13.refs_2_), channel_id=1, source_target_pairs={{0,2},{2,0},{1,3},{3,1},{4,6},{6,4},{5,7},{7,5},{8,10},{10,8},{9,1... | collective-permute-start | bytes 202760 | tf_op jit(solution)/shard_map/ppermute | solution.py:40
  8.0 3.6 %collective-permute-start.1 = (bf16[1,264,128]{2,1,0:T(8,128)(2,1)S(1)}, bf16[1,264,128]{2,1,0:T(8,128)(2,1)S(1)}, u32[]{:S(2)}, u32[]{:S(2)}) collective-permute-start(bf16[1,264,128]{2,1,0:T(8,128)(2,1)S(1)} %get-tuple-element.13.refs_2_), channel_id=1, source_target_pairs={{0,1},{1,0},{2,3},{3,2},{4,5},{5,4},{6,7},{7,6},{8,9},{9,8},{10,11... | collective-permute-start | bytes 202760 | tf_op jit(solution)/shard_map/ppermute | solution.py:40
  8.3 4.5 %collective-permute-start.10 = (bf16[1,264,128]{2,1,0:T(8,128)(2,1)S(1)}, bf16[1,264,128]{2,1,0:T(8,128)(2,1)S(1)}, u32[]{:S(2)}, u32[]{:S(2)}) collective-permute-start(bf16[1,264,128]{2,1,0:T(8,128)(2,1)S(1)} %collective-permute-done.2.refs_4_), channel_id=1, source_target_pairs={{0,2},{2,0},{1,3},{3,1},{4,6},{6,4},{5,7},{7,5},{8,10},{10,8},{9,1... | collective-permute-start | bytes 202760 | tf_op jit(solution)/shard_map/ppermute | solution.py:40
  10.1 4.4 %collective-permute-start.3 = (bf16[1,264,128]{2,1,0:T(8,128)(2,1)S(1)}, bf16[1,264,128]{2,1,0:T(8,128)(2,1)S(1)}, u32[]{:S(2)}, u32[]{:S(2)}) collective-permute-start(bf16[1,264,128]{2,1,0:T(8,128)(2,1)S(1)} %collective-permute-done.2.refs_4_), channel_id=1, source_target_pairs={{0,1},{1,0},{2,3},{3,2},{4,5},{5,4},{6,7},{7,6},{8,9},{9,8},{10,11... | collective-permute-start | bytes 202760 | tf_op jit(solution)/shard_map/ppermute | solution.py:40
  11.3 3.6 %collective-permute-start.12 = (bf16[1,264,128]{2,1,0:T(8,128)(2,1)S(1)}, bf16[1,264,128]{2,1,0:T(8,128)(2,1)S(1)}, u32[]{:S(2)}, u32[]{:S(2)}) collective-permute-start(bf16[1,264,128]{2,1,0:T(8,128)(2,1)S(1)} %collective-permute-done.4.refs_6_), channel_id=1, source_target_pairs={{0,2},{2,0},{1,3},{3,1},{4,6},{6,4},{5,7},{7,5},{8,10},{10,8},{9,1... | collective-permute-start | bytes 202760 | tf_op jit(solution)/shard_map/ppermute | solution.py:40
  11.6 6.1 %collective-permute-start.5 = (bf16[1,264,128]{2,1,0:T(8,128)(2,1)S(1)}, bf16[1,264,128]{2,1,0:T(8,128)(2,1)S(1)}, u32[]{:S(2)}, u32[]{:S(2)}) collective-permute-start(bf16[1,264,128]{2,1,0:T(8,128)(2,1)S(1)} %collective-permute-done.4.refs_6_), channel_id=1, source_target_pairs={{0,1},{1,0},{2,3},{3,2},{4,5},{5,4},{6,7},{7,6},{8,9},{9,8},{10,11... | collective-permute-start | bytes 202760 | tf_op jit(solution)/shard_map/ppermute | solution.py:40
  12.8 4.8 %collective-permute-start.14 = (bf16[1,264,128]{2,1,0:T(8,128)(2,1)S(1)}, bf16[1,264,128]{2,1,0:T(8,128)(2,1)S(1)}, u32[]{:S(2)}, u32[]{:S(2)}) collective-permute-start(bf16[1,264,128]{2,1,0:T(8,128)(2,1)S(1)} %collective-permute-done.6.refs_8_), channel_id=1, source_target_pairs={{0,2},{2,0},{1,3},{3,1},{4,6},{6,4},{5,7},{7,5},{8,10},{10,8},{9,1... | collective-permute-start | bytes 202760 | tf_op jit(solution)/shard_map/ppermute | solution.py:40
  14.6 3.8 %collective-permute-start.7 = (bf16[1,264,128]{2,1,0:T(8,128)(2,1)S(1)}, bf16[1,264,128]{2,1,0:T(8,128)(2,1)S(1)}, u32[]{:S(2)}, u32[]{:S(2)}) collective-permute-start(bf16[1,264,128]{2,1,0:T(8,128)(2,1)S(1)} %collective-permute-done.6.refs_8_), channel_id=1, source_target_pairs={{0,1},{1,0},{2,3},{3,2},{4,5},{5,4},{6,7},{7,6},{8,9},{9,8},{10,11... | collective-permute-start | bytes 202760 | tf_op jit(solution)/shard_map/ppermute | solution.py:40
  14.9 3.6 %collective-permute-start.9 = (bf16[1,264,128]{2,1,0:T(8,128)(2,1)S(1)}, bf16[1,264,128]{2,1,0:T(8,128)(2,1)S(1)}, u32[]{:S(2)}, u32[]{:S(2)}) collective-permute-start(bf16[1,264,128]{2,1,0:T(8,128)(2,1)S(1)} %collective-permute-done.8.refs_10_), channel_id=1, source_target_pairs={{0,1},{1,0},{2,3},{3,2},{4,5},{5,4},{6,7},{7,6},{8,9},{9,8},{10,11... | collective-permute-start | bytes 202760 | tf_op jit(solution)/shard_map/ppermute | solution.py:40
  17.7 1.3 %collective-permute-start.11 = (bf16[1,264,128]{2,1,0:T(8,128)(2,1)S(1)}, bf16[1,264,128]{2,1,0:T(8,128)(2,1)S(1)}, u32[]{:S(2)}, u32[]{:S(2)}) collective-permute-start(bf16[1,264,128]{2,1,0:T(8,128)(2,1)S(1)} %collective-permute-done.10.refs_12_), channel_id=1, source_target_pairs={{0,1},{1,0},{2,3},{3,2},{4,5},{5,4},{6,7},{7,6},{8,9},{9,8},{10,11... | collective-permute-start | bytes 202760 | tf_op jit(solution)/shard_map/ppermute | solution.py:40
  17.7 1.6 %collective-permute-start.13 = (bf16[1,264,128]{2,1,0:T(8,128)(2,1)S(1)}, bf16[1,264,128]{2,1,0:T(8,128)(2,1)S(1)}, u32[]{:S(2)}, u32[]{:S(2)}) collective-permute-start(bf16[1,264,128]{2,1,0:T(8,128)(2,1)S(1)} %collective-permute-done.12.refs_14_), channel_id=1, source_target_pairs={{0,1},{1,0},{2,3},{3,2},{4,5},{5,4},{6,7},{7,6},{8,9},{9,8},{10,11... | collective-permute-start | bytes 202760 | tf_op jit(solution)/shard_map/ppermute | solution.py:40
  18.4 1.3 %collective-permute-start.15 = (bf16[1,264,128]{2,1,0:T(8,128)(2,1)S(1)}, bf16[1,264,128]{2,1,0:T(8,128)(2,1)S(1)}, u32[]{:S(2)}, u32[]{:S(2)}) collective-permute-start(bf16[1,264,128]{2,1,0:T(8,128)(2,1)S(1)} %collective-permute-done.14.refs_16_), channel_id=1, source_target_pairs={{0,1},{1,0},{2,3},{3,2},{4,5},{5,4},{6,7},{7,6},{8,9},{9,8},{10,11... | collective-permute-start | bytes 202760 | tf_op jit(solution)/shard_map/ppermute | solution.py:40
  24.0 5.0 %collective-permute-start.18 = (bf16[1,8,32,128]{3,2,1,0:T(8,128)(2,1)S(1)}, bf16[1,8,32,128]{3,2,1,0:T(8,128)(2,1)S(1)}, u32[]{:S(2)}, u32[]{:S(2)}) collective-permute-start(bf16[1,8,32,128]{3,2,1,0:T(8,128)(2,1)S(1)} %get-tuple-element.20), channel_id=1, source_target_pairs={{0,4},{4,8},{8,12},{12,0},{1,5},{5,9},{9,13},{13,1},{2,6},{6,10},{... | collective-permute-start | bytes 196616 | tf_op jit(solution)/shard_map/ppermute | solution.py:40
  24.7 6.5 %collective-permute-start.16 = (bf16[1,8,32,128]{3,2,1,0:T(8,128)(2,1)S(1)}, bf16[1,8,32,128]{3,2,1,0:T(8,128)(2,1)S(1)}, u32[]{:S(2)}, u32[]{:S(2)}) collective-permute-start(bf16[1,8,32,128]{3,2,1,0:T(8,128)(2,1)S(1)} %get-tuple-element.17), channel_id=1, source_target_pairs={{0,8},{4,12},{8,0},{12,4},{1,9},{5,13},{9,1},{13,5},{2,10},{6,14},... | collective-permute-start | bytes 196616 | tf_op jit(solution)/shard_map/ppermute | solution.py:40
  27.6 6.7 %collective-permute-start.17 = (bf16[1,8,32,128]{3,2,1,0:T(8,128)(2,1)S(1)}, bf16[1,8,32,128]{3,2,1,0:T(8,128)(2,1)S(1)}, u32[]{:S(2)}, u32[]{:S(2)}) collective-permute-start(bf16[1,8,32,128]{3,2,1,0:T(8,128)(2,1)S(1)} %get-tuple-element.18), channel_id=1, source_target_pairs={{0,12},{4,0},{8,4},{12,8},{1,13},{5,1},{9,5},{13,9},{2,14},{6,2},{... | collective-permute-start | bytes 196616 | tf_op jit(solution)/shard_map/ppermute | solution.py:40
